TPU v7x, 32 devices: a whole 2x2x4 slice. The times are simulated.
32 devices in a mesh: groups: 2 (over y), offset: 4 (over x, core), space: 4 (over z).
Axes of the slice: x: 2, y: 2, z: 4, core: 2. Of those that a mesh axis runs over, the one named last changes fastest.
Arguments:
- src_now: float32 [4, 256, 2048], P('offset', ('groups', 'space')), parts along dimension 1, may hold values from -6 to 6
- src_prev: float32 [4, 256, 2048], P('offset', ('groups', 'space')), parts along dimension 1, may hold values from -6 to 6
- rcv_now: float32 [4, 256, 2048], P('offset', ('groups', 'space')), parts along dimension 1, may hold values from -6 to 6
- rcv_prev: float32 [4, 256, 2048], P('offset', ('groups', 'space')), parts along dimension 1, may hold values from -6 to 6
- courant: float32 [256, 2048], P(('groups', 'space')), parts along dimension 0, may hold values from 0.05 to 0.2
- shot_cell: int32 [8], P('groups'), parts along dimension 0, may hold values from 0 to 262143
- wavelet: float32 [8], P('groups'), parts along dimension 0, may hold values from 4 to 8
- shifts: int32 [128], replicated, may hold values from -64 to 64
- angle_map: float32 [128, 128], replicated, may hold values from -0.5 to 0.5
Outputs:
- angle_image: float32 [128, 256, 2048], P(None, ('groups', 'space'), 'offset'), parts along dimension 1
There are 2 independent parts, one for each index of `groups`. A program takes and returns all parts, laid end to end along the dimension named above; an argument that names none is the same for every part. Nothing has to cross between parts.
All inputs are finite; a program needn't handle non-finite values.
Results may differ from a plain program's by a relative error of at most 0.0003.
Values sent between devices are 32-bit elements; how exact they have to be, the bound alone decides.
No kernel may reach another device: no remote copies, remote signals or barrier semaphores. Data moves between devices by JAX's collectives and lax.ppermute only.
A program may use at most 128 MiB of HBM per device.

v0:
```python
import functools

import jax
import jax.numpy as jnp
from jax import lax
from jax.experimental import pallas as pl
from jax.experimental.pallas import tpu as pltpu
from jax.sharding import PartitionSpec as P

MAXLAG = 64
LANES = 128
ROWS = 2 * LANES
GROUP = 8
RIM = 4
PITCH = LANES + 1
MB = 4
NB = 4
MARGIN = 8

coeffs = (-205.0 / 72.0, 8.0 / 5.0, -1.0 / 5.0, 8.0 / 315.0, -1.0 / 560.0)


def split(x):
    high = x.astype(jnp.bfloat16)
    low = (x - high.astype(jnp.float32)).astype(jnp.bfloat16)
    return high, low


def edge_body(src_top, src_low, rcv_top, rcv_low, up_ref, down_ref):
    up_ref[0:RIM, :] = src_top[0, 0:RIM, :]
    up_ref[RIM : 2 * RIM, :] = rcv_top[0, 0:RIM, :]
    down_ref[0:RIM, :] = src_low[0, GROUP - RIM : GROUP, :]
    down_ref[RIM : 2 * RIM, :] = rcv_low[0, GROUP - RIM : GROUP, :]


def edge_rows(src_now, rcv_now):
    depth, nx = src_now.shape[1:]
    top = pl.BlockSpec((1, GROUP, nx), lambda i: (0, 0, 0))
    low = pl.BlockSpec((1, GROUP, nx), lambda i: (0, depth // GROUP - 1, 0))
    return pl.pallas_call(
        edge_body,
        grid=(1,),
        in_specs=[top, low, top, low],
        out_specs=[pl.BlockSpec((GROUP, nx), lambda i: (0, 0))] * 2,
        out_shape=[jax.ShapeDtypeStruct((GROUP, nx), jnp.float32)] * 2,
        name="edge_rows",
    )(src_now, src_now, rcv_now, rcv_now)


def stepped(ext, prev, courant, rows):
    nx = ext.shape[1]
    cols = lax.broadcasted_iota(jnp.int32, (rows, nx), 1)
    now = ext[RIM : RIM + rows, :]
    total = (2.0 * coeffs[0]) * now
    for k in range(1, RIM + 1):
        left = jnp.where(cols < k, 0.0, pltpu.roll(now, k, 1))
        right = jnp.where(cols >= nx - k, 0.0, pltpu.roll(now, nx - k, 1))
        total = total + coeffs[k] * (ext[RIM - k : RIM - k + rows, :] + ext[RIM + k : RIM + k + rows, :] + left + right)
    return 2.0 * now - prev + courant * total


def injected(value, first_row, nx, cell, amp):
    rows = lax.broadcasted_iota(jnp.int32, value.shape, 0) + first_row
    flat = rows * nx + lax.broadcasted_iota(jnp.int32, value.shape, 1)
    return value + jnp.where(flat == cell, amp, 0.0)


def spread(padded, outs, width):
    me = lax.axis_index("offset")
    for d, out in enumerate(outs):
        first = pl.multiple_of(lax.bitwise_xor(me, d) * width, LANES)
        out[...] = padded[:, :, pl.ds(first, width + 2 * MAXLAG)]


def place(padded, f, row, value):
    rows, nx = value.shape
    zero = jnp.zeros((rows, MAXLAG), jnp.float32)
    padded[f, row : row + rows, :] = jnp.concatenate([zero, value, zero], 1)


def inner_body(width, cell_ref, amp_ref, src_now, src_prev, rcv_now, rcv_prev, courant, *refs):
    outs, padded = refs[:-1], refs[-1]
    depth, nx = src_now.shape[1:]
    me = lax.axis_index("offset")
    slab = lax.axis_index("space") * depth
    for f, (now, prev) in enumerate(((src_now, src_prev), (rcv_now, rcv_prev))):
        for z in range(GROUP, depth - GROUP, GROUP):
            value = stepped(now[0, z - RIM : z + GROUP + RIM, :], prev[0, z : z + GROUP, :], courant[z : z + GROUP, :], GROUP)
            if f == 0:
                value = injected(value, slab + z, nx, cell_ref[me], amp_ref[me])
            place(padded, f, z - GROUP, value)
    spread(padded, outs, width)


def outer_body(width, cell_ref, amp_ref, above, below, src_now, src_prev, rcv_now, rcv_prev, courant, *refs):
    outs, padded = refs[:-1], refs[-1]
    depth, nx = src_now.shape[1:]
    me = lax.axis_index("offset")
    slab = lax.axis_index("space") * depth
    for f, (now, prev) in enumerate(((src_now, src_prev), (rcv_now, rcv_prev))):
        for b, z in enumerate((0, depth - GROUP)):
            if b == 0:
                ext = jnp.concatenate([above[f * RIM : (f + 1) * RIM, :], now[0, 0 : GROUP + RIM, :]], 0)
            else:
                ext = jnp.concatenate([now[0, depth - GROUP - RIM : depth, :], below[f * RIM : (f + 1) * RIM, :]], 0)
            value = stepped(ext, prev[0, z : z + GROUP, :], courant[z : z + GROUP, :], GROUP)
            if f == 0:
                value = injected(value, slab + z, nx, cell_ref[me], amp_ref[me])
            place(padded, f, b * GROUP, value)
    spread(padded, outs, width)


def windows(body, name, count, rows, halos, cell, amp, fields):
    nx = fields[0].shape[2]
    width = nx // count
    out = jax.ShapeDtypeStruct((2, rows, width + 2 * MAXLAG), jnp.float32)
    smem = pl.BlockSpec(memory_space=pltpu.SMEM)
    vmem = pl.BlockSpec(memory_space=pltpu.VMEM)
    return pl.pallas_call(
        functools.partial(body, width),
        in_specs=[smem, smem] + [vmem] * (len(halos) + len(fields)),
        out_specs=[vmem] * count,
        out_shape=[out] * count,
        scratch_shapes=[pltpu.VMEM((2, rows, nx + 2 * MAXLAG), jnp.float32)],
        name=name,
    )(cell, amp, *halos, *fields)


def weight_body(shift_ref, map_ref, mw_ref, slot_ref):
    lag = lax.broadcasted_iota(jnp.int32, (ROWS, LANES), 0) - MAXLAG
    hot = jnp.where(lag == shift_ref[...], 1.0, 0.0)
    full = lax.dot_general(
        map_ref[...], hot, (((1,), (1,)), ((), ())), precision=lax.Precision.HIGHEST, preferred_element_type=jnp.float32
    )
    na = full.shape[0]
    used = jnp.max(hot[:LANES, :], axis=1, keepdims=True)
    k = lax.broadcasted_iota(jnp.int32, (LANES, 1), 0).astype(jnp.float32)
    slot = jnp.min(jnp.where(used > 0.0, float(ROWS), k), axis=0, keepdims=True).astype(jnp.int32)
    column = lax.broadcasted_iota(jnp.int32, (na, LANES), 1)
    w = jnp.where(column == slot, full[:, LANES : LANES + 1], full[:, :LANES])
    high, low = split(w)
    mw_ref[0, :, :LANES] = high
    mw_ref[0, :, LANES:] = high
    mw_ref[1, :, :LANES] = low
    mw_ref[1, :, LANES:] = jnp.zeros_like(low)
    slot_ref[...] = jnp.broadcast_to(slot, slot_ref.shape)


def angle_weights(shifts, angle_map):
    na = angle_map.shape[0]
    return pl.pallas_call(
        weight_body,
        out_shape=[jax.ShapeDtypeStruct((2, na, ROWS), jnp.bfloat16), jax.ShapeDtypeStruct((GROUP, LANES), jnp.int32)],
        name="angle_weights",
    )(shifts.reshape(1, -1), angle_map)


def products(na, shots, slot_ref, mw_ref, fwd, rev, obuf, rhs):
    slot = slot_ref[...]
    sub = lax.broadcasted_iota(jnp.int32, (GROUP, LANES), 0)
    steps = 16 // MB

    def fill(rho, mb, buf):
        extra = []
        for m in range(mb * MB, (mb + 1) * MB):
            tot = None
            for s in range(shots):
                t = rev[s, pl.ds(ROWS - 1 - 8 * m - rho, 1), :] * fwd[s, pl.ds(LANES + 8 * m + rho, 1), :]
                tot = t if tot is None else tot + t
            extra.append(jnp.broadcast_to(tot, (GROUP, LANES)))
        for nb in range(16 // NB):
            acc = [[None] * NB for _ in range(MB)]
            for s in range(shots):
                a = {}
                c = {}
                for i in range(MB):
                    for j in range(NB):
                        m, n = mb * MB + i, nb * NB + j
                        if n - m not in a:
                            a[n - m] = rev[s, pl.ds(LANES - 1 - rho + 8 * (n - m), GROUP), :]
                        if n + m not in c:
                            c[n + m] = fwd[s, pl.ds(rho + 8 * (n + m), GROUP), :]
                        t = a[n - m] * c[n + m]
                        acc[i][j] = t if acc[i][j] is None else acc[i][j] + t
            for j in range(0, NB, 2):
                n = nb * NB + j
                masks = [sub == slot - 8 * (n + k) for k in range(2)]
                for i in range(MB):
                    high, low = split(jnp.concatenate([jnp.where(masks[k], extra[i], acc[i][j + k]) for k in range(2)], 0))
                    rhs[buf, 8 * n : 8 * n + 16, i * LANES : (i + 1) * LANES] = high
                    rhs[buf, LANES + 8 * n : LANES + 8 * n + 16, i * LANES : (i + 1) * LANES] = low

    def contract(rho, mb, buf):
        res = jnp.dot(mw_ref[0], rhs[buf], preferred_element_type=jnp.float32)
        res += jnp.dot(mw_ref[1], rhs[buf], preferred_element_type=jnp.float32)
        for i in range(MB):
            obuf[pl.ds(MARGIN + 8 * (mb * MB + i) + rho, na, stride=PITCH), :] = res[:, i * LANES : (i + 1) * LANES]

    @pl.loop(0, 8)
    def _(rho):
        contract(rho - 1, steps - 1, (steps - 1) % 2)
        for mb in range(steps):
            fill(rho, mb, mb % 2)
            if mb:
                contract(rho, mb - 1, (mb - 1) % 2)

    contract(7, steps - 1, (steps - 1) % 2)


def image_body(blocks, ablk, shots, slot_ref, mw_ref, *refs):
    inner, outer = refs[:shots], refs[shots : 2 * shots]
    out_ref, fwd, rev, obuf = refs[2 * shots :]
    depth = out_ref.shape[1]

    @pl.when(pl.program_id(0) == 0)
    def _():
        rows = lax.broadcasted_iota(jnp.int32, (LANES, LANES), 0)
        cols = lax.broadcasted_iota(jnp.int32, (LANES, LANES), 1)
        anti = (rows + cols == LANES - 1).astype(jnp.float32)

        def gathered(s, f, b):
            tiles = []
            for q in range(blocks):
                at = slice((q + b) * LANES, (q + b + 1) * LANES)
                tiles += [outer[s][f, :GROUP, at], inner[s][f, :, at], outer[s][f, GROUP:, at]]
            if blocks * depth < LANES:
                tiles.append(jnp.zeros((LANES - blocks * depth, LANES), jnp.float32))
            return jnp.concatenate(tiles, 0)

        for s in range(shots):
            for b in range(2):
                fwd[s, b * LANES : (b + 1) * LANES, :] = gathered(s, 1, b).T
                rev[s, (1 - b) * LANES : (2 - b) * LANES, :] = lax.dot_general(
                    anti, gathered(s, 0, b), (((1,), (1,)), ((), ())),
                    precision=lax.Precision.HIGHEST, preferred_element_type=jnp.float32)

        pl.run_scoped(
            functools.partial(products, mw_ref.shape[1], shots, slot_ref, mw_ref, fwd, rev, obuf),
            pltpu.VMEM((2, ROWS, LANES * MB), jnp.bfloat16),
        )

    first = pl.program_id(0) * ablk
    for a in range(ablk):
        tile = obuf[pl.ds(MARGIN + (first + a) * PITCH, LANES), :].T
        for q in range(blocks):
            out_ref[a, :, q * LANES : (q + 1) * LANES] = tile[q * depth : (q + 1) * depth, :]


def angle_image(inner, outer, mw, slot, depth):
    shots = len(inner)
    full = inner[0].shape[2]
    width = full - 2 * MAXLAG
    na = mw.shape[1]
    ablk = 16
    whole = lambda x: pl.BlockSpec(x.shape, lambda i: (0,) * x.ndim)
    return pl.pallas_call(
        functools.partial(image_body, width // LANES, ablk, shots),
        out_shape=jax.ShapeDtypeStruct((na, depth, width), jnp.float32),
        grid=(na // ablk,),
        in_specs=[whole(slot), whole(mw)] + [whole(x) for x in inner + outer],
        out_specs=pl.BlockSpec((ablk, depth, width), lambda i: (i, 0, 0)),
        scratch_shapes=[
            pltpu.VMEM((shots, ROWS, LANES), jnp.float32),
            pltpu.VMEM((shots, ROWS, LANES), jnp.float32),
            pltpu.VMEM((2 * MARGIN + na * PITCH, LANES), jnp.float32),
        ],
        compiler_params=pltpu.CompilerParams(vmem_limit_bytes=56 << 20),
        name="angle_image",
    )(slot, mw, *inner, *outer)


def body(src_now, src_prev, rcv_now, rcv_prev, courant, shot_cell, wavelet, shifts, angle_map):
    depth = src_now.shape[1]
    count = lax.axis_size("offset")
    slabs = lax.axis_size("space")
    fields = (src_now, src_prev, rcv_now, rcv_prev, courant)
    up, down = edge_rows(src_now, rcv_now)
    below = lax.ppermute(up, "space", [(i + 1, i) for i in range(slabs - 1)])
    above = lax.ppermute(down, "space", [(i, i + 1) for i in range(slabs - 1)])

    def exchanged(wins):
        return [wins[0]] + [lax.ppermute(wins[d], "offset", [(i, i ^ d) for i in range(count)]) for d in range(1, count)]

    inner = exchanged(windows(inner_body, "inner_rows", count, depth - 2 * GROUP, (), shot_cell, wavelet, fields))
    outer = exchanged(windows(outer_body, "outer_rows", count, 2 * GROUP, (above, below), shot_cell, wavelet, fields))
    mw, slot = angle_weights(shifts, angle_map)
    return angle_image(inner, outer, mw, slot, depth)


def solution(mesh):
    placed = (
        P("offset", ("groups", "space"), None),
        P("offset", ("groups", "space"), None),
        P("offset", ("groups", "space"), None),
        P("offset", ("groups", "space"), None),
        P(("groups", "space"), None),
        P("groups"),
        P("groups"),
        P(),
        P(),
    )
    step = jax.shard_map(
        body,
        mesh=mesh,
        in_specs=placed,
        out_specs=P(None, ("groups", "space"), "offset"),
        check_vma=False,
    )

    def run(*args):
        with jax.sharding.use_abstract_mesh(mesh.abstract_mesh):
            return step(*args)

    return run
```

profile of v0, /device:TPU:0, one launch (start us, length us, event | category | flops | bytes accessed | tf_op | source)
XLA Modules:
  0.0 41.9 jit_solution(1824057625563443648)
XLA Ops:
  0.0 3.0 %inner_rows.1 = (f32[2,16,640]{2,1,0:T(8,128)}, f32[2,16,640]{2,1,0:T(8,128)}, f32[2,16,640]{2,1,0:T(8,128)}, f32[2,16,640]{2,1,0:T(8,128)}) custom-call(s32[4]{0:T(128)} %cell_ref.3, f32[4]{0:T(128)} %amp_ref.3, f32[1,32,2048]{2,1,0:T(8,128)} %src_now.3, f32[1,32,2048]{2,1,0:T(8,128)} %src_prev.3, f32[1,32,2048]{2,1,0:T(8,128)} %rcv_now.3, ...), custom_call_target="tpu_custom_call" | custom-call | tf_op jit(solution)/shard_map/inner_rows/pallas_call | solution.py:119
  3.0 0.5 %collective-permute-start = (f32[2,16,640]{2,1,0:T(8,128)}, f32[2,16,640]{2,1,0:T(8,128)S(1)}, u32[]{:S(2)}, u32[]{:S(2)}) collective-permute-start(f32[2,16,640]{2,1,0:T(8,128)} %get-tuple-element.20), channel_id=1, source_target_pairs={{0,4},{4,0},{8,12},{12,8},{1,5},{5,1},{9,13},{13,9},{2,6},{6,2},{1... | collective-permute-start | bytes 245768 | tf_op jit(solution)/shard_map/ppermute | solution.py:282
  3.5 1.6 %edge_rows.1 = (f32[8,2048]{1,0:T(8,128)}, f32[8,2048]{1,0:T(8,128)}) custom-call(f32[1,32,2048]{2,1,0:T(8,128)} %src_now.3, f32[1,32,2048]{2,1,0:T(8,128)} %src_now.3, f32[1,32,2048]{2,1,0:T(8,128)} %rcv_now.3, f32[1,32,2048]{2,1,0:T(8,128)} %rcv_now.3), custom_call_target="tpu_custom_call" | custom-call | tf_op jit(solution)/shard_map/edge_rows/pallas_call | solution.py:40
  5.1 4.5 %collective-permute-start.3 = (f32[8,2048]{1,0:T(8,128)}, f32[8,2048]{1,0:T(8,128)S(1)}, u32[]{:S(2)}, u32[]{:S(2)}) collective-permute-start(f32[8,2048]{1,0:T(8,128)} %get-tuple-element.23), channel_id=1, source_target_pairs={{0,1},{1,2},{2,3},{4,5},{5,6},{6,7},{8,9},{9,10},{10,11},{12,13},{... | collective-permute-start | bytes 196616 | tf_op jit(solution)/shard_map/ppermute | solution.py:279
  9.6 1.3 %collective-permute-start.4 = (f32[8,2048]{1,0:T(8,128)}, f32[8,2048]{1,0:T(8,128)S(1)}, u32[]{:S(2)}, u32[]{:S(2)}) collective-permute-start(f32[8,2048]{1,0:T(8,128)} %get-tuple-element.24), channel_id=1, source_target_pairs={{1,0},{2,1},{3,2},{5,4},{6,5},{7,6},{9,8},{10,9},{11,10},{13,12},{... | collective-permute-start | bytes 196616 | tf_op jit(solution)/shard_map/ppermute | solution.py:278
  10.9 1.6 %collective-permute-start.1 = (f32[2,16,640]{2,1,0:T(8,128)}, f32[2,16,640]{2,1,0:T(8,128)S(1)}, u32[]{:S(2)}, u32[]{:S(2)}) collective-permute-start(f32[2,16,640]{2,1,0:T(8,128)} %get-tuple-element.21), channel_id=1, source_target_pairs={{0,8},{4,12},{8,0},{12,4},{1,9},{5,13},{9,1},{13,5},{2,10},{6,14},... | collective-permute-start | bytes 245768 | tf_op jit(solution)/shard_map/ppermute | solution.py:282
  12.4 0.1 collective-permute-start.2
  12.5 0.0 collective-permute-done.3.above
  12.5 0.0 copy-start.6
  12.5 3.4 %collective-permute-done.4.below = f32[8,2048]{1,0:T(8,128)S(1)} collective-permute-done((f32[8,2048]{1,0:T(8,128)}, f32[8,2048]{1,0:T(8,128)S(1)}, u32[]{:S(2)}, u32[]{:S(2)}) %collective-permute-start.4) | collective-permute-done | bytes 65568 | tf_op jit(solution)/shard_map/ppermute | solution.py:278
  16.0 0.0 copy-done.6
  16.0 0.0 copy-start.7
  16.0 0.6 %copy-done.7 = f32[8,2048]{1,0:T(8,128)} copy-done((f32[8,2048]{1,0:T(8,128)}, f32[8,2048]{1,0:T(8,128)S(1)}, u32[]{:S(2)}) %copy-start.7) | copy-done | bytes 65560
  16.6 3.2 %outer_rows.1 = (f32[2,16,640]{2,1,0:T(8,128)}, f32[2,16,640]{2,1,0:T(8,128)}, f32[2,16,640]{2,1,0:T(8,128)}, f32[2,16,640]{2,1,0:T(8,128)}) custom-call(s32[4]{0:T(128)} %cell_ref.3, f32[4]{0:T(128)} %amp_ref.3, f32[8,2048]{1,0:T(8,128)} %copy-done.6, f32[8,2048]{1,0:T(8,128)} %copy-done.7, f32[1,32,2048]{2,1,0:T(8,128)} %src_now.3, ...), custom_call_target="tpu_custom_call" | custom-call | tf_op jit(solution)/shard_map/outer_rows/pallas_call | solution.py:119
  19.7 0.0 collective-permute-start.5
  19.7 1.5 %collective-permute-start.6 = (f32[2,16,640]{2,1,0:T(8,128)}, f32[2,16,640]{2,1,0:T(8,128)S(1)}, u32[]{:S(2)}, u32[]{:S(2)}) collective-permute-start(f32[2,16,640]{2,1,0:T(8,128)} %get-tuple-element.27), channel_id=1, source_target_pairs={{0,8},{4,12},{8,0},{12,4},{1,9},{5,13},{9,1},{13,5},{2,10},{6,14},... | collective-permute-start | bytes 245768 | tf_op jit(solution)/shard_map/ppermute | solution.py:282
  21.3 0.0 collective-permute-done.refs_1_
  21.3 0.0 copy-start
  21.3 0.3 collective-permute-start.7
  21.6 1.9 %angle_weights.1 = (bf16[2,128,256]{2,1,0:T(8,128)(2,1)}, s32[8,128]{1,0:T(8,128)}) custom-call(s32[1,128]{1,0:T(1,128)} %bitcast.1, f32[128,128]{1,0:T(8,128)} %map_ref.1), custom_call_target="tpu_custom_call" | custom-call | tf_op jit(solution)/shard_map/angle_weights/pallas_call | solution.py:151
  23.5 0.0 collective-permute-done.1.refs_2_
  23.5 0.0 copy-start.1
  23.5 0.0 collective-permute-done.2.refs_3_
  23.5 0.0 copy-start.2
  23.5 0.0 collective-permute-done.5.refs_5_
  23.5 0.0 copy-start.3
  23.5 1.6 %collective-permute-done.6.refs_6_ = f32[2,16,640]{2,1,0:T(8,128)S(1)} collective-permute-done((f32[2,16,640]{2,1,0:T(8,128)}, f32[2,16,640]{2,1,0:T(8,128)S(1)}, u32[]{:S(2)}, u32[]{:S(2)}) %collective-permute-start.6) | collective-permute-done | bytes 81952 | tf_op jit(solution)/shard_map/ppermute | solution.py:282
  25.1 0.0 copy-start.4
  25.1 1.1 %collective-permute-done.7.refs_7_ = f32[2,16,640]{2,1,0:T(8,128)S(1)} collective-permute-done((f32[2,16,640]{2,1,0:T(8,128)}, f32[2,16,640]{2,1,0:T(8,128)S(1)}, u32[]{:S(2)}, u32[]{:S(2)}) %collective-permute-start.7) | collective-permute-done | bytes 81952 | tf_op jit(solution)/shard_map/ppermute | solution.py:282
  26.2 0.0 copy-start.5
  26.3 0.0 copy-done
  26.3 0.0 copy-done.1
  26.3 0.0 copy-done.2
  26.3 0.0 copy-done.3
  26.3 0.0 copy-done.4
  26.3 0.6 %copy-done.5 = f32[2,16,640]{2,1,0:T(8,128)} copy-done((f32[2,16,640]{2,1,0:T(8,128)}, f32[2,16,640]{2,1,0:T(8,128)S(1)}, u32[]{:S(2)}) %copy-start.5) | copy-done | bytes 81944
  26.9 15.0 %angle_image.1 = f32[128,32,512]{2,1,0:T(8,128)} custom-call(s32[8,128]{1,0:T(8,128)} %get-tuple-element.17.slot_ref, bf16[2,128,256]{2,1,0:T(8,128)(2,1)} %get-tuple-element.18.mw_ref, f32[2,16,640]{2,1,0:T(8,128)} %get-tuple-element.19.refs_0_, f32[2,16,640]{2,1,0:T(8,128)} %copy-done, f32[2,16,640]{2,1,0:T(8,128)} %copy-done.1, f32[2,16,640]{2,1,0:T(8,128)} %copy-done.2, ...), custom_call_target="tpu_custom_call" | custom-call | tf_op jit(solution)/shard_map/angle_image/pallas_call | solution.py:256
Async XLA Ops:
  3.0 18.3 %collective-permute-start = (f32[2,16,640]{2,1,0:T(8,128)}, f32[2,16,640]{2,1,0:T(8,128)S(1)}, u32[]{:S(2)}, u32[]{:S(2)}) collective-permute-start(f32[2,16,640]{2,1,0:T(8,128)} %get-tuple-element.20), channel_id=1, source_target_pairs={{0,4},{4,0},{8,12},{12,8},{1,5},{5,1},{9,13},{13,9},{2,6},{6,2},{1... | collective-permute-start | bytes 245768 | tf_op jit(solution)/shard_map/ppermute | solution.py:282
  5.1 7.4 %collective-permute-start.3 = (f32[8,2048]{1,0:T(8,128)}, f32[8,2048]{1,0:T(8,128)S(1)}, u32[]{:S(2)}, u32[]{:S(2)}) collective-permute-start(f32[8,2048]{1,0:T(8,128)} %get-tuple-element.23), channel_id=1, source_target_pairs={{0,1},{1,2},{2,3},{4,5},{5,6},{6,7},{8,9},{9,10},{10,11},{12,13},{... | collective-permute-start | bytes 196616 | tf_op jit(solution)/shard_map/ppermute | solution.py:279
  9.6 6.4 %collective-permute-start.4 = (f32[8,2048]{1,0:T(8,128)}, f32[8,2048]{1,0:T(8,128)S(1)}, u32[]{:S(2)}, u32[]{:S(2)}) collective-permute-start(f32[8,2048]{1,0:T(8,128)} %get-tuple-element.24), channel_id=1, source_target_pairs={{1,0},{2,1},{3,2},{5,4},{6,5},{7,6},{9,8},{10,9},{11,10},{13,12},{... | collective-permute-start | bytes 196616 | tf_op jit(solution)/shard_map/ppermute | solution.py:278
  10.9 12.6 %collective-permute-start.1 = (f32[2,16,640]{2,1,0:T(8,128)}, f32[2,16,640]{2,1,0:T(8,128)S(1)}, u32[]{:S(2)}, u32[]{:S(2)}) collective-permute-start(f32[2,16,640]{2,1,0:T(8,128)} %get-tuple-element.21), channel_id=1, source_target_pairs={{0,8},{4,12},{8,0},{12,4},{1,9},{5,13},{9,1},{13,5},{2,10},{6,14},... | collective-permute-start | bytes 245768 | tf_op jit(solution)/shard_map/ppermute | solution.py:282
  12.4 11.0 %collective-permute-start.2 = (f32[2,16,640]{2,1,0:T(8,128)}, f32[2,16,640]{2,1,0:T(8,128)S(1)}, u32[]{:S(2)}, u32[]{:S(2)}) collective-permute-start(f32[2,16,640]{2,1,0:T(8,128)} %get-tuple-element.22), channel_id=1, source_target_pairs={{0,12},{4,8},{8,4},{12,0},{1,13},{5,9},{9,5},{13,1},{2,14},{6,10},... | collective-permute-start | bytes 245768 | tf_op jit(solution)/shard_map/ppermute | solution.py:282
  12.5 3.4 %copy-start.6 = (f32[8,2048]{1,0:T(8,128)}, f32[8,2048]{1,0:T(8,128)S(1)}, u32[]{:S(2)}) copy-start(f32[8,2048]{1,0:T(8,128)S(1)} %collective-permute-done.3.above) | copy-start | bytes 196612
  16.0 0.6 %copy-start.7 = (f32[8,2048]{1,0:T(8,128)}, f32[8,2048]{1,0:T(8,128)S(1)}, u32[]{:S(2)}) copy-start(f32[8,2048]{1,0:T(8,128)S(1)} %collective-permute-done.4.below) | copy-start | bytes 196612
  19.7 3.8 %collective-permute-start.5 = (f32[2,16,640]{2,1,0:T(8,128)}, f32[2,16,640]{2,1,0:T(8,128)S(1)}, u32[]{:S(2)}, u32[]{:S(2)}) collective-permute-start(f32[2,16,640]{2,1,0:T(8,128)} %get-tuple-element.26), channel_id=1, source_target_pairs={{0,4},{4,0},{8,12},{12,8},{1,5},{5,1},{9,13},{13,9},{2,6},{6,2},{1... | collective-permute-start | bytes 245768 | tf_op jit(solution)/shard_map/ppermute | solution.py:282
  19.7 5.4 %collective-permute-start.6 = (f32[2,16,640]{2,1,0:T(8,128)}, f32[2,16,640]{2,1,0:T(8,128)S(1)}, u32[]{:S(2)}, u32[]{:S(2)}) collective-permute-start(f32[2,16,640]{2,1,0:T(8,128)} %get-tuple-element.27), channel_id=1, source_target_pairs={{0,8},{4,12},{8,0},{12,4},{1,9},{5,13},{9,1},{13,5},{2,10},{6,14},... | collective-permute-start | bytes 245768 | tf_op jit(solution)/shard_map/ppermute | solution.py:282
  21.3 5.0 %copy-start = (f32[2,16,640]{2,1,0:T(8,128)}, f32[2,16,640]{2,1,0:T(8,128)S(1)}, u32[]{:S(2)}) copy-start(f32[2,16,640]{2,1,0:T(8,128)S(1)} %collective-permute-done.refs_1_) | copy-start | bytes 245764
  21.3 5.0 %collective-permute-start.7 = (f32[2,16,640]{2,1,0:T(8,128)}, f32[2,16,640]{2,1,0:T(8,128)S(1)}, u32[]{:S(2)}, u32[]{:S(2)}) collective-permute-start(f32[2,16,640]{2,1,0:T(8,128)} %get-tuple-element.28), channel_id=1, source_target_pairs={{0,12},{4,8},{8,4},{12,0},{1,13},{5,9},{9,5},{13,1},{2,14},{6,10},... | collective-permute-start | bytes 245768 | tf_op jit(solution)/shard_map/ppermute | solution.py:282
  23.5 2.8 %copy-start.1 = (f32[2,16,640]{2,1,0:T(8,128)}, f32[2,16,640]{2,1,0:T(8,128)S(1)}, u32[]{:S(2)}) copy-start(f32[2,16,640]{2,1,0:T(8,128)S(1)} %collective-permute-done.1.refs_2_) | copy-start | bytes 245764
  23.5 2.8 %copy-start.2 = (f32[2,16,640]{2,1,0:T(8,128)}, f32[2,16,640]{2,1,0:T(8,128)S(1)}, u32[]{:S(2)}) copy-start(f32[2,16,640]{2,1,0:T(8,128)S(1)} %collective-permute-done.2.refs_3_) | copy-start | bytes 245764
  23.5 2.8 %copy-start.3 = (f32[2,16,640]{2,1,0:T(8,128)}, f32[2,16,640]{2,1,0:T(8,128)S(1)}, u32[]{:S(2)}) copy-start(f32[2,16,640]{2,1,0:T(8,128)S(1)} %collective-permute-done.5.refs_5_) | copy-start | bytes 245764
  25.1 1.1 %copy-start.4 = (f32[2,16,640]{2,1,0:T(8,128)}, f32[2,16,640]{2,1,0:T(8,128)S(1)}, u32[]{:S(2)}) copy-start(f32[2,16,640]{2,1,0:T(8,128)S(1)} %collective-permute-done.6.refs_6_) | copy-start | bytes 245764
  26.2 0.6 %copy-start.5 = (f32[2,16,640]{2,1,0:T(8,128)}, f32[2,16,640]{2,1,0:T(8,128)S(1)}, u32[]{:S(2)}) copy-start(f32[2,16,640]{2,1,0:T(8,128)S(1)} %collective-permute-done.7.refs_7_) | copy-start | bytes 245764
where the time goes:
time: 42.2 us; the launch traced here: 41.9 us
  Pallas kernels  24.6 us (58%)
  starting transfers between devices  9.75 us (23%)
  waiting for transfers between devices  6.16 us (15%)
  local copies, waits for them, and re-layouts  1.25 us (3%)
    pallas_call x1, Pallas kernels, angle_image(): pl.pallas_call(functools.partial(image_body, width // LANES, ablk, shots)...  15 us
    pallas_call x2, Pallas kernels, windows(): pl.pallas_call(functools.partial(body, width), in_specs=[smem, smem] + [v...  6.16 us
    ppermute x1, starting transfers between devices, body(): above = lax.ppermute(down, 'space', [(i, i + 1) for i in range(slabs - 1)])  4.46 us
    ppermute x6, starting transfers between devices, exchanged(): lax.ppermute(wins[d], 'offset', [(i, i ^ d) for i in range(count)])  4 us
    ppermute x1, waiting for transfers between devices, body(): below = lax.ppermute(up, 'space', [(i + 1, i) for i in range(slabs - 1)])  3.42 us
    ppermute x6, waiting for transfers between devices, exchanged(): lax.ppermute(wins[d], 'offset', [(i, i ^ d) for i in range(count)])  2.74 us
    pallas_call x1, Pallas kernels, angle_weights(): pl.pallas_call(weight_body, out_shape=[jax.ShapeDtypeStruct((2, na, ROWS)...  1.86 us
    pallas_call x1, Pallas kernels, edge_rows(): pl.pallas_call(edge_body, grid=(1,), in_specs=[top, low, top, low], out_s...  1.62 us
  transfers between devices with their start and end apart: 8, of which 3 were waited for; matrix products, arithmetic and copies ran while one was open for 0% of the time, Pallas kernels for 16%

commit v1 on v0

v1 whole, which is shorter than its diff:
```python
import functools

import jax
import jax.numpy as jnp
from jax import lax
from jax.experimental import pallas as pl
from jax.experimental.pallas import tpu as pltpu
from jax.sharding import PartitionSpec as P

MAXLAG = 64
LANES = 128
ROWS = 2 * LANES
GROUP = 8
RIM = 4
PITCH = LANES + 1
MB = 4
NB = 4
APART = 16

coeffs = (-205.0 / 72.0, 8.0 / 5.0, -1.0 / 5.0, 8.0 / 315.0, -1.0 / 560.0)


def split(x):
    high = x.astype(jnp.bfloat16)
    low = (x - high.astype(jnp.float32)).astype(jnp.bfloat16)
    return high, low


def lateral(tiles, lane):
    zero = jnp.zeros_like(tiles[0])
    total = [None] * len(tiles)
    for k in range(1, RIM + 1):
        up = [pltpu.roll(v, k, 1) for v in tiles]
        down = [pltpu.roll(v, LANES - k, 1) for v in tiles]
        for t in range(len(tiles)):
            left = jnp.where(lane < k, up[t - 1] if t else zero, up[t])
            right = jnp.where(lane >= LANES - k, down[t + 1] if t + 1 < len(tiles) else zero, down[t])
            term = coeffs[k] * (left + right)
            total[t] = term if total[t] is None else total[t] + term
    return total


def step_rows(jobs, width, cell_ref, amp_ref, prevs, courant, rows_ref, padded, outs):
    pitch = rows_ref.shape[2]
    count = len(outs)
    nx = courant.shape[1]
    depth = courant.shape[0]
    blocks = nx // LANES
    me = lax.axis_index("offset")
    cell = cell_ref[me] - lax.axis_index("space") * depth * nx
    amp = amp_ref[me]
    lane = lax.broadcasted_iota(jnp.int32, (GROUP, LANES), 1)
    flat = lax.broadcasted_iota(jnp.int32, (GROUP, LANES), 0) * nx + lane
    source = lax.broadcasted_iota(jnp.int32, (LANES, LANES), 0)
    target = lax.broadcasted_iota(jnp.int32, (LANES, LANES), 1)
    mirror = (lax.rem(source + target + 1, LANES) == MAXLAG).astype(jnp.float32)
    half = lane < MAXLAG
    zero = jnp.zeros((GROUP, LANES), jnp.float32)
    for f in range(2):
        for row, z in jobs:
            tiles = [rows_ref[f, t, z + RIM : z + RIM + GROUP, :] for t in range(blocks)]
            across = lateral(tiles, lane)
            out = []
            for t in range(blocks):
                at = slice(t * LANES, (t + 1) * LANES)
                total = (2.0 * coeffs[0]) * tiles[t] + across[t]
                for k in range(1, RIM + 1):
                    total = total + coeffs[k] * (
                        rows_ref[f, t, z + RIM - k : z + RIM - k + GROUP, :] + rows_ref[f, t, z + RIM + k : z + RIM + k + GROUP, :]
                    )
                value = 2.0 * tiles[t] - prevs[f][0, z : z + GROUP, at] + courant[z : z + GROUP, at] * total
                if f == 0:
                    value = value + jnp.where(flat == cell - (z * nx + t * LANES), amp, 0.0)
                out.append(value)
            if f == 0:
                turned = jnp.dot(
                    jnp.concatenate(out[::-1], 0), mirror, precision=lax.Precision.HIGHEST, preferred_element_type=jnp.float32
                )
                out = [turned[t * GROUP : (t + 1) * GROUP, :] for t in range(blocks)]
            else:
                out = [pltpu.roll(v, MAXLAG, 1) for v in out]
            out = [zero] + out + [zero]
            for t in range(blocks + 1):
                padded[f, row : row + GROUP, t * LANES : (t + 1) * LANES] = jnp.where(half, out[t], out[t + 1])
    for d, out in enumerate(outs):
        other = lax.bitwise_xor(me, d)
        for f, first in enumerate((count - 1 - other, other)):
            out[f] = padded[f, :, pl.ds(pl.multiple_of(first * width, LANES), width + 2 * MAXLAG)]


def inner_body(width, cell_ref, amp_ref, src_now, src_prev, rcv_now, rcv_prev, courant, up_ref, down_ref, *refs):
    outs, rows_ref, padded = refs[:-2], refs[-2], refs[-1]
    depth, nx = src_now.shape[1:]
    for f, now in enumerate((src_now, rcv_now)):
        up_ref[f * RIM : (f + 1) * RIM, :] = now[0, 0:RIM, :]
        down_ref[f * RIM : (f + 1) * RIM, :] = now[0, depth - RIM : depth, :]
        for t in range(nx // LANES):
            rows_ref[f, t, RIM : RIM + depth, :] = now[0, :, t * LANES : (t + 1) * LANES]
    jobs = [(z - GROUP, z) for z in range(GROUP, depth - GROUP, GROUP)]
    step_rows(jobs, width, cell_ref, amp_ref, (src_prev, rcv_prev), courant, rows_ref, padded, outs)


def outer_body(width, cell_ref, amp_ref, above, below, src_now, src_prev, rcv_now, rcv_prev, courant, *refs):
    outs, rows_ref, padded = refs[:-2], refs[-2], refs[-1]
    depth, nx = src_now.shape[1:]
    for f, now in enumerate((src_now, rcv_now)):
        for t in range(nx // LANES):
            at = slice(t * LANES, (t + 1) * LANES)
            rows_ref[f, t, 0:RIM, :] = above[f * RIM : (f + 1) * RIM, at]
            rows_ref[f, t, RIM : RIM + 2 * GROUP, :] = now[0, 0 : 2 * GROUP, at]
            rows_ref[f, t, RIM + depth - 2 * GROUP : RIM + depth, :] = now[0, depth - 2 * GROUP : depth, at]
            rows_ref[f, t, RIM + depth : 2 * RIM + depth, :] = below[f * RIM : (f + 1) * RIM, at]
    jobs = [(0, 0), (GROUP, depth - GROUP)]
    step_rows(jobs, width, cell_ref, amp_ref, (src_prev, rcv_prev), courant, rows_ref, padded, outs)


def windows(body, name, count, rows, halos, extra, cell, amp, fields):
    depth, nx = fields[0].shape[1:]
    width = nx // count
    out = jax.ShapeDtypeStruct((2, rows, width + 2 * MAXLAG), jnp.float32)
    smem = pl.BlockSpec(memory_space=pltpu.SMEM)
    vmem = pl.BlockSpec(memory_space=pltpu.VMEM)
    return pl.pallas_call(
        functools.partial(body, width),
        in_specs=[smem, smem] + [vmem] * (len(halos) + len(fields)),
        out_specs=[vmem] * (len(extra) + count),
        out_shape=extra + [out] * count,
        scratch_shapes=[
            pltpu.VMEM((2, nx // LANES, depth + 2 * RIM, LANES), jnp.float32),
            pltpu.VMEM((2, rows, nx + 2 * MAXLAG), jnp.float32),
        ],
        name=name,
    )(cell, amp, *halos, *fields)


def weight_body(shift_ref, map_ref, mw_ref, slot_ref):
    lag = lax.broadcasted_iota(jnp.int32, (ROWS, LANES), 0) - MAXLAG
    hot = jnp.where(lag == shift_ref[...], 1.0, 0.0)
    full = lax.dot_general(
        map_ref[...], hot, (((1,), (1,)), ((), ())), precision=lax.Precision.HIGHEST, preferred_element_type=jnp.float32
    )
    na = full.shape[0]
    used = jnp.max(hot[:LANES, :], axis=1, keepdims=True)
    k = lax.broadcasted_iota(jnp.int32, (LANES, 1), 0).astype(jnp.float32)
    slot = jnp.min(jnp.where(used > 0.0, float(ROWS), k), axis=0, keepdims=True).astype(jnp.int32)
    column = lax.broadcasted_iota(jnp.int32, (na, LANES), 1)
    w = jnp.where(column == slot, full[:, LANES : LANES + 1], full[:, :LANES])
    high, low = split(w)
    mw_ref[0, :, :LANES] = high
    mw_ref[0, :, LANES:] = high
    mw_ref[1, :, :LANES] = low
    mw_ref[1, :, LANES:] = jnp.zeros_like(low)
    slot_ref[...] = jnp.broadcast_to(slot, slot_ref.shape)


def angle_weights(shifts, angle_map):
    na = angle_map.shape[0]
    return pl.pallas_call(
        weight_body,
        out_shape=[jax.ShapeDtypeStruct((2, na, ROWS), jnp.bfloat16), jax.ShapeDtypeStruct((GROUP, LANES), jnp.int32)],
        name="angle_weights",
    )(shifts.reshape(1, -1), angle_map)


def products(na, shots, slot_ref, mw_ref, fwd, rev, obuf, rhs):
    slot = slot_ref[...]
    sub = lax.broadcasted_iota(jnp.int32, (GROUP, LANES), 0)
    steps = 16 // MB

    def fill(rho, mb, buf):
        extra = []
        for m in range(mb * MB, (mb + 1) * MB):
            tot = None
            for s in range(shots):
                t = rev[s, pl.ds(ROWS - 1 - 8 * m - rho, 1), :] * fwd[s, pl.ds(LANES + 8 * m + rho, 1), :]
                tot = t if tot is None else tot + t
            extra.append(jnp.broadcast_to(tot, (GROUP, LANES)))
        for nb in range(16 // NB):
            acc = [[None] * NB for _ in range(MB)]
            for s in range(shots):
                a = {}
                c = {}
                for i in range(MB):
                    for j in range(NB):
                        m, n = mb * MB + i, nb * NB + j
                        if n - m not in a:
                            a[n - m] = rev[s, pl.ds(LANES - 1 - rho + 8 * (n - m), GROUP), :]
                        if n + m not in c:
                            c[n + m] = fwd[s, pl.ds(rho + 8 * (n + m), GROUP), :]
                        t = a[n - m] * c[n + m]
                        acc[i][j] = t if acc[i][j] is None else acc[i][j] + t
            for j in range(0, NB, 2):
                n = nb * NB + j
                masks = [sub == slot - 8 * (n + k) for k in range(2)]
                for i in range(MB):
                    high, low = split(jnp.concatenate([jnp.where(masks[k], extra[i], acc[i][j + k]) for k in range(2)], 0))
                    rhs[buf, 8 * n : 8 * n + 16, i * LANES : (i + 1) * LANES] = high
                    rhs[buf, LANES + 8 * n : LANES + 8 * n + 16, i * LANES : (i + 1) * LANES] = low

    def contract(rho, mb, buf):
        res = jnp.dot(mw_ref[0], rhs[buf], preferred_element_type=jnp.float32)
        res += jnp.dot(mw_ref[1], rhs[buf], preferred_element_type=jnp.float32)
        for i in range(MB):
            obuf[pl.ds(8 * (mb * MB + i) + rho, na, stride=PITCH), :] = res[:, i * LANES : (i + 1) * LANES]

    items = [(rho, mb) for rho in range(GROUP) for mb in range(steps)]
    for i, (rho, mb) in enumerate(items):
        fill(rho, mb, i % 2)
        if i:
            contract(*items[i - 1], (i - 1) % 2)
    contract(*items[-1], (len(items) - 1) % 2)


def image_body(blocks, shots, slot_ref, mw_ref, *refs):
    sent = refs[: 2 * shots]
    out_ref, held, fwd, rev, obuf, stage, in_sems, out_sems = refs[2 * shots :]
    na, depth, _ = out_ref.shape
    fetches = [pltpu.make_async_copy(sent[i], held.at[i], in_sems.at[i]) for i in range(2 * shots)]
    for fetch in fetches:
        fetch.start()

    def gathered(s, f, b):
        inner, outer = held.at[s], held.at[shots + s]
        tiles = []
        for q in range(blocks):
            t = q + b if f else blocks - 1 - q + b
            at = slice(t * LANES, (t + 1) * LANES)
            tiles += [outer[f, :GROUP, at], inner[f, :, at], outer[f, GROUP:, at]]
        if blocks * depth < LANES:
            tiles.append(jnp.zeros((LANES - blocks * depth, LANES), jnp.float32))
        return jnp.concatenate(tiles, 0)

    for fetch in fetches:
        fetch.wait()
    for s in range(shots):
        for b in range(2):
            fwd[s, b * LANES : (b + 1) * LANES, :] = gathered(s, 1, b).T
            rev[s, b * LANES : (b + 1) * LANES, :] = gathered(s, 0, b).T

    pl.run_scoped(
        functools.partial(products, na, shots, slot_ref, mw_ref, fwd, rev, obuf),
        pltpu.VMEM((2, ROWS, LANES * MB), jnp.bfloat16),
    )

    def leave(i):
        at = pl.ds(i * APART, APART)
        return pltpu.make_async_copy(stage.at[at], out_ref.at[at], out_sems.at[i])

    @pl.loop(0, na // (2 * APART))
    def _(i):
        for part in range(2):
            for a in range(APART):
                angle = (2 * i + part) * APART + a
                tile = obuf[pl.ds(angle * PITCH, LANES), :].T
                for q in range(blocks):
                    stage[angle, :, q * LANES : (q + 1) * LANES] = tile[q * depth : (q + 1) * depth, :]
            leave(2 * i + part).start()

    @pl.loop(0, na // APART)
    def _(i):
        leave(i).wait()


def angle_image(inner, outer, mw, slot, depth):
    shots = len(inner)
    full = inner[0].shape[2]
    width = full - 2 * MAXLAG
    na = mw.shape[1]
    vmem = pl.BlockSpec(memory_space=pltpu.VMEM)
    anywhere = pl.BlockSpec(memory_space=pl.ANY)
    return pl.pallas_call(
        functools.partial(image_body, width // LANES, shots),
        out_shape=jax.ShapeDtypeStruct((na, depth, width), jnp.float32),
        in_specs=[vmem, vmem] + [anywhere] * (2 * shots),
        out_specs=anywhere,
        scratch_shapes=[
            pltpu.VMEM((2 * shots, *inner[0].shape), jnp.float32),
            pltpu.VMEM((shots, ROWS, LANES), jnp.float32),
            pltpu.VMEM((shots, ROWS, LANES), jnp.float32),
            pltpu.VMEM((na * PITCH, LANES), jnp.float32),
            pltpu.VMEM((na, depth, width), jnp.float32),
            pltpu.SemaphoreType.DMA((2 * shots,)),
            pltpu.SemaphoreType.DMA((na // APART,)),
        ],
        compiler_params=pltpu.CompilerParams(vmem_limit_bytes=40 << 20),
        name="angle_image",
    )(slot, mw, *inner, *outer)


def body(src_now, src_prev, rcv_now, rcv_prev, courant, shot_cell, wavelet, shifts, angle_map):
    depth = src_now.shape[1]
    count = lax.axis_size("offset")
    slabs = lax.axis_size("space")
    fields = (src_now, src_prev, rcv_now, rcv_prev, courant)
    edge = jax.ShapeDtypeStruct((2 * RIM, src_now.shape[2]), jnp.float32)

    def exchanged(wins):
        return [wins[0]] + [lax.ppermute(wins[d], "offset", [(i, i ^ d) for i in range(count)]) for d in range(1, count)]

    up, down, *inner = windows(
        inner_body, "inner_rows", count, depth - 2 * GROUP, (), [edge, edge], shot_cell, wavelet, fields
    )
    below = lax.ppermute(up, "space", [(i + 1, i) for i in range(slabs - 1)])
    above = lax.ppermute(down, "space", [(i, i + 1) for i in range(slabs - 1)])
    inner = exchanged(inner)
    outer = exchanged(windows(outer_body, "outer_rows", count, 2 * GROUP, (above, below), [], shot_cell, wavelet, fields))
    mw, slot = angle_weights(shifts, angle_map)
    return angle_image(inner, outer, mw, slot, depth)


def solution(mesh):
    placed = (
        P("offset", ("groups", "space"), None),
        P("offset", ("groups", "space"), None),
        P("offset", ("groups", "space"), None),
        P("offset", ("groups", "space"), None),
        P(("groups", "space"), None),
        P("groups"),
        P("groups"),
        P(),
        P(),
    )
    step = jax.shard_map(
        body,
        mesh=mesh,
        in_specs=placed,
        out_specs=P(None, ("groups", "space"), "offset"),
        check_vma=False,
    )

    def run(*args):
        with jax.sharding.use_abstract_mesh(mesh.abstract_mesh):
            return step(*args)

    return run
```

time: 42.2 us -> 38.1 us (0.903)
  Pallas kernels: 24.6 us -> 17.8 us
  local copies, waits for them, and re-layouts: 1.25 us -> 3.97 us
    pallas_call x2 -> x1, Pallas kernels: 16.6 us -> 10.1 us  [angle_image(): pl.pallas_call(functools.partial(image_body, width // LANES, shots), out_...]
    unnamed x16 -> x12, local copies, waits for them, and re-layouts: 1.25 us -> 3.97 us
  transfers between devices with their start and end apart: 8 -> 8, of which waited for: 3 -> 3; matrix products, arithmetic and copies ran while one was open for 0% -> 0% of each run, Pallas kernels for 16% -> 13%
where the time goes in v1:
time: 38.1 us; the launch traced here: 37.8 us
  Pallas kernels  17.8 us (47%)
  starting transfers between devices  9.75 us (26%)
  waiting for transfers between devices  6.19 us (16%)
  local copies, waits for them, and re-layouts  3.97 us (10%)
    pallas_call x1, Pallas kernels, angle_image(): pl.pallas_call(functools.partial(image_body, width // LANES, shots), out_...  10.1 us
    pallas_call x2, Pallas kernels, windows(): pl.pallas_call(functools.partial(body, width), in_specs=[smem, smem] + [v...  5.86 us
    ppermute x1, starting transfers between devices, body(): above = lax.ppermute(down, 'space', [(i, i + 1) for i in range(slabs - 1)])  4.46 us
    ppermute x6, starting transfers between devices, exchanged(): lax.ppermute(wins[d], 'offset', [(i, i ^ d) for i in range(count)])  3.99 us
    unnamed x12, local copies, waits for them, and re-layouts  3.97 us
    ppermute x1, waiting for transfers between devices, body(): below = lax.ppermute(up, 'space', [(i + 1, i) for i in range(slabs - 1)])  3.42 us
    ppermute x6, waiting for transfers between devices, exchanged(): lax.ppermute(wins[d], 'offset', [(i, i ^ d) for i in range(count)])  2.76 us
    pallas_call x1, Pallas kernels, angle_weights(): pl.pallas_call(weight_body, out_shape=[jax.ShapeDtypeStruct((2, na, ROWS)...  1.87 us
  transfers between devices with their start and end apart: 8, of which 3 were waited for; matrix products, arithmetic and copies ran while one was open for 0% of the time, Pallas kernels for 13%

profile of v1, /device:TPU:0, one launch (start us, length us, event | category | flops | bytes accessed | tf_op | source)
XLA Modules:
  0.0 37.8 jit_solution(3394091407725382101)
XLA Ops:
  0.0 2.9 %inner_rows.1 = (f32[8,2048]{1,0:T(8,128)}, f32[8,2048]{1,0:T(8,128)}, f32[2,16,640]{2,1,0:T(8,128)}, f32[2,16,640]{2,1,0:T(8,128)}, f32[2,16,640]{2,1,0:T(8,128)}, /*index=5*/f32[2,16,640]{2,1,0:T(8,128)}) custom-call(s32[4]{0:T(128)} %cell_ref.3, f32[4]{0:T(128)} %amp_ref.3, f32[1,32,2048]{2,1,0:T(8,128)} %src_now.3, f32[1,32,2048]{2,1,0:T(8,128)} %src_prev.3, ...), custom_call_target="tpu_custom_call" | custom-call | tf_op jit(solution)/shard_map/inner_rows/pallas_call | solution.py:123
  2.9 0.5 %collective-permute-start = (f32[2,16,640]{2,1,0:T(8,128)}, f32[2,16,640]{2,1,0:T(8,128)S(1)}, u32[]{:S(2)}, u32[]{:S(2)}) collective-permute-start(f32[2,16,640]{2,1,0:T(8,128)} %get-tuple-element.20), channel_id=1, source_target_pairs={{0,4},{4,0},{8,12},{12,8},{1,5},{5,1},{9,13},{13,9},{2,6},{6,2},{1... | collective-permute-start | bytes 245768 | tf_op jit(solution)/shard_map/ppermute | solution.py:298
  3.4 4.5 %collective-permute-start.3 = (f32[8,2048]{1,0:T(8,128)}, f32[8,2048]{1,0:T(8,128)S(1)}, u32[]{:S(2)}, u32[]{:S(2)}) collective-permute-start(f32[8,2048]{1,0:T(8,128)} %get-tuple-element.23), channel_id=1, source_target_pairs={{0,1},{1,2},{2,3},{4,5},{5,6},{6,7},{8,9},{9,10},{10,11},{12,13},{... | collective-permute-start | bytes 196616 | tf_op jit(solution)/shard_map/ppermute | solution.py:304
  7.8 1.3 %collective-permute-start.4 = (f32[8,2048]{1,0:T(8,128)}, f32[8,2048]{1,0:T(8,128)S(1)}, u32[]{:S(2)}, u32[]{:S(2)}) collective-permute-start(f32[8,2048]{1,0:T(8,128)} %get-tuple-element.24), channel_id=1, source_target_pairs={{1,0},{2,1},{3,2},{5,4},{6,5},{7,6},{9,8},{10,9},{11,10},{13,12},{... | collective-permute-start | bytes 196616 | tf_op jit(solution)/shard_map/ppermute | solution.py:303
  9.1 1.6 %collective-permute-start.1 = (f32[2,16,640]{2,1,0:T(8,128)}, f32[2,16,640]{2,1,0:T(8,128)S(1)}, u32[]{:S(2)}, u32[]{:S(2)}) collective-permute-start(f32[2,16,640]{2,1,0:T(8,128)} %get-tuple-element.21), channel_id=1, source_target_pairs={{0,8},{4,12},{8,0},{12,4},{1,9},{5,13},{9,1},{13,5},{2,10},{6,14},... | collective-permute-start | bytes 245768 | tf_op jit(solution)/shard_map/ppermute | solution.py:298
  10.7 0.1 collective-permute-start.2
  10.8 0.0 collective-permute-done.3.above
  10.8 0.0 copy-start.4
  10.8 3.4 %collective-permute-done.4.below = f32[8,2048]{1,0:T(8,128)S(1)} collective-permute-done((f32[8,2048]{1,0:T(8,128)}, f32[8,2048]{1,0:T(8,128)S(1)}, u32[]{:S(2)}, u32[]{:S(2)}) %collective-permute-start.4) | collective-permute-done | bytes 65568 | tf_op jit(solution)/shard_map/ppermute | solution.py:303
  14.2 0.0 copy-done.4
  14.2 0.0 copy-start.5
  14.2 0.6 %copy-done.5 = f32[8,2048]{1,0:T(8,128)} copy-done((f32[8,2048]{1,0:T(8,128)}, f32[8,2048]{1,0:T(8,128)S(1)}, u32[]{:S(2)}) %copy-start.5) | copy-done | bytes 65560
  14.8 3.0 %outer_rows.1 = (f32[2,16,640]{2,1,0:T(8,128)}, f32[2,16,640]{2,1,0:T(8,128)}, f32[2,16,640]{2,1,0:T(8,128)}, f32[2,16,640]{2,1,0:T(8,128)}) custom-call(s32[4]{0:T(128)} %cell_ref.3, f32[4]{0:T(128)} %amp_ref.3, f32[8,2048]{1,0:T(8,128)} %copy-done.4, f32[8,2048]{1,0:T(8,128)} %copy-done.5, f32[1,32,2048]{2,1,0:T(8,128)} %src_now.3, ...), custom_call_target="tpu_custom_call" | custom-call | tf_op jit(solution)/shard_map/outer_rows/pallas_call | solution.py:123
  17.8 0.0 collective-permute-start.5
  17.8 1.5 %collective-permute-start.6 = (f32[2,16,640]{2,1,0:T(8,128)}, f32[2,16,640]{2,1,0:T(8,128)S(1)}, u32[]{:S(2)}, u32[]{:S(2)}) collective-permute-start(f32[2,16,640]{2,1,0:T(8,128)} %get-tuple-element.27), channel_id=1, source_target_pairs={{0,8},{4,12},{8,0},{12,4},{1,9},{5,13},{9,1},{13,5},{2,10},{6,14},... | collective-permute-start | bytes 245768 | tf_op jit(solution)/shard_map/ppermute | solution.py:298
  19.4 0.0 collective-permute-done.refs_1_
  19.4 0.3 collective-permute-start.7
  19.7 1.9 %angle_weights.1 = (bf16[2,128,256]{2,1,0:T(8,128)(2,1)}, s32[8,128]{1,0:T(8,128)}) custom-call(s32[1,128]{1,0:T(1,128)} %bitcast.1, f32[128,128]{1,0:T(8,128)} %map_ref.1), custom_call_target="tpu_custom_call" | custom-call | tf_op jit(solution)/shard_map/angle_weights/pallas_call | solution.py:158
  21.5 0.0 collective-permute-done.1.refs_2_
  21.6 0.0 collective-permute-done.2.refs_3_
  21.6 0.0 collective-permute-done.5.refs_5_
  21.6 1.6 %collective-permute-done.6.refs_6_ = f32[2,16,640]{2,1,0:T(8,128)S(1)} collective-permute-done((f32[2,16,640]{2,1,0:T(8,128)}, f32[2,16,640]{2,1,0:T(8,128)S(1)}, u32[]{:S(2)}, u32[]{:S(2)}) %collective-permute-start.6) | collective-permute-done | bytes 81952 | tf_op jit(solution)/shard_map/ppermute | solution.py:298
  23.2 1.1 %collective-permute-done.7.refs_7_ = f32[2,16,640]{2,1,0:T(8,128)S(1)} collective-permute-done((f32[2,16,640]{2,1,0:T(8,128)}, f32[2,16,640]{2,1,0:T(8,128)S(1)}, u32[]{:S(2)}, u32[]{:S(2)}) %collective-permute-start.7) | collective-permute-done | bytes 81952 | tf_op jit(solution)/shard_map/ppermute | solution.py:298
  24.3 0.0 copy-start
  24.3 0.9 %copy-done = bf16[2,128,256]{2,1,0:T(8,128)(2,1)S(1)} copy-done((bf16[2,128,256]{2,1,0:T(8,128)(2,1)S(1)}, bf16[2,128,256]{2,1,0:T(8,128)(2,1)}, u32[]{:S(2)}) %copy-start) | copy-done | bytes 131096
  25.2 0.0 copy-start.1
  25.2 0.9 %copy-done.1 = f32[2,16,640]{2,1,0:T(8,128)S(1)} copy-done((f32[2,16,640]{2,1,0:T(8,128)S(1)}, f32[2,16,640]{2,1,0:T(8,128)}, u32[]{:S(2)}) %copy-start.1) | copy-done | bytes 81944
  26.1 0.0 copy-start.2
  26.1 0.9 %copy-done.2 = f32[2,16,640]{2,1,0:T(8,128)S(1)} copy-done((f32[2,16,640]{2,1,0:T(8,128)S(1)}, f32[2,16,640]{2,1,0:T(8,128)}, u32[]{:S(2)}) %copy-start.2) | copy-done | bytes 81944
  27.0 0.0 copy-start.3
  27.0 0.7 %copy-done.3 = s32[8,128]{1,0:T(8,128)S(1)} copy-done((s32[8,128]{1,0:T(8,128)S(1)}, s32[8,128]{1,0:T(8,128)}, u32[]{:S(2)}) %copy-start.3) | copy-done | bytes 4120
  27.7 10.1 %angle_image.1 = f32[128,32,512]{2,1,0:T(8,128)} custom-call(s32[8,128]{1,0:T(8,128)S(1)} %copy-done.3, bf16[2,128,256]{2,1,0:T(8,128)(2,1)S(1)} %copy-done, f32[2,16,640]{2,1,0:T(8,128)S(1)} %copy-done.1, f32[2,16,640]{2,1,0:T(8,128)S(1)} %collective-permute-done.refs_1_, f32[2,16,640]{2,1,0:T(8,128)S(1)} %collective-permute-done.1.refs_2_, ...), custom_call_target="tpu_custom_call" | custom-call | tf_op jit(solution)/shard_map/angle_image/pallas_call | solution.py:271
Async XLA Ops:
  2.9 16.5 %collective-permute-start = (f32[2,16,640]{2,1,0:T(8,128)}, f32[2,16,640]{2,1,0:T(8,128)S(1)}, u32[]{:S(2)}, u32[]{:S(2)}) collective-permute-start(f32[2,16,640]{2,1,0:T(8,128)} %get-tuple-element.20), channel_id=1, source_target_pairs={{0,4},{4,0},{8,12},{12,8},{1,5},{5,1},{9,13},{13,9},{2,6},{6,2},{1... | collective-permute-start | bytes 245768 | tf_op jit(solution)/shard_map/ppermute | solution.py:298
  3.4 7.4 %collective-permute-start.3 = (f32[8,2048]{1,0:T(8,128)}, f32[8,2048]{1,0:T(8,128)S(1)}, u32[]{:S(2)}, u32[]{:S(2)}) collective-permute-start(f32[8,2048]{1,0:T(8,128)} %get-tuple-element.23), channel_id=1, source_target_pairs={{0,1},{1,2},{2,3},{4,5},{5,6},{6,7},{8,9},{9,10},{10,11},{12,13},{... | collective-permute-start | bytes 196616 | tf_op jit(solution)/shard_map/ppermute | solution.py:304
  7.8 6.4 %collective-permute-start.4 = (f32[8,2048]{1,0:T(8,128)}, f32[8,2048]{1,0:T(8,128)S(1)}, u32[]{:S(2)}, u32[]{:S(2)}) collective-permute-start(f32[8,2048]{1,0:T(8,128)} %get-tuple-element.24), channel_id=1, source_target_pairs={{1,0},{2,1},{3,2},{5,4},{6,5},{7,6},{9,8},{10,9},{11,10},{13,12},{... | collective-permute-start | bytes 196616 | tf_op jit(solution)/shard_map/ppermute | solution.py:303
  9.1 12.4 %collective-permute-start.1 = (f32[2,16,640]{2,1,0:T(8,128)}, f32[2,16,640]{2,1,0:T(8,128)S(1)}, u32[]{:S(2)}, u32[]{:S(2)}) collective-permute-start(f32[2,16,640]{2,1,0:T(8,128)} %get-tuple-element.21), channel_id=1, source_target_pairs={{0,8},{4,12},{8,0},{12,4},{1,9},{5,13},{9,1},{13,5},{2,10},{6,14},... | collective-permute-start | bytes 245768 | tf_op jit(solution)/shard_map/ppermute | solution.py:298
  10.7 10.8 %collective-permute-start.2 = (f32[2,16,640]{2,1,0:T(8,128)}, f32[2,16,640]{2,1,0:T(8,128)S(1)}, u32[]{:S(2)}, u32[]{:S(2)}) collective-permute-start(f32[2,16,640]{2,1,0:T(8,128)} %get-tuple-element.22), channel_id=1, source_target_pairs={{0,12},{4,8},{8,4},{12,0},{1,13},{5,9},{9,5},{13,1},{2,14},{6,10},... | collective-permute-start | bytes 245768 | tf_op jit(solution)/shard_map/ppermute | solution.py:298
  10.8 3.4 %copy-start.4 = (f32[8,2048]{1,0:T(8,128)}, f32[8,2048]{1,0:T(8,128)S(1)}, u32[]{:S(2)}) copy-start(f32[8,2048]{1,0:T(8,128)S(1)} %collective-permute-done.3.above) | copy-start | bytes 196612
  14.2 0.6 %copy-start.5 = (f32[8,2048]{1,0:T(8,128)}, f32[8,2048]{1,0:T(8,128)S(1)}, u32[]{:S(2)}) copy-start(f32[8,2048]{1,0:T(8,128)S(1)} %collective-permute-done.4.below) | copy-start | bytes 196612
  17.8 3.7 %collective-permute-start.5 = (f32[2,16,640]{2,1,0:T(8,128)}, f32[2,16,640]{2,1,0:T(8,128)S(1)}, u32[]{:S(2)}, u32[]{:S(2)}) collective-permute-start(f32[2,16,640]{2,1,0:T(8,128)} %get-tuple-element.26), channel_id=1, source_target_pairs={{0,4},{4,0},{8,12},{12,8},{1,5},{5,1},{9,13},{13,9},{2,6},{6,2},{1... | collective-permute-start | bytes 245768 | tf_op jit(solution)/shard_map/ppermute | solution.py:298
  17.8 5.4 %collective-permute-start.6 = (f32[2,16,640]{2,1,0:T(8,128)}, f32[2,16,640]{2,1,0:T(8,128)S(1)}, u32[]{:S(2)}, u32[]{:S(2)}) collective-permute-start(f32[2,16,640]{2,1,0:T(8,128)} %get-tuple-element.27), channel_id=1, source_target_pairs={{0,8},{4,12},{8,0},{12,4},{1,9},{5,13},{9,1},{13,5},{2,10},{6,14},... | collective-permute-start | bytes 245768 | tf_op jit(solution)/shard_map/ppermute | solution.py:298
  19.4 5.0 %collective-permute-start.7 = (f32[2,16,640]{2,1,0:T(8,128)}, f32[2,16,640]{2,1,0:T(8,128)S(1)}, u32[]{:S(2)}, u32[]{:S(2)}) collective-permute-start(f32[2,16,640]{2,1,0:T(8,128)} %get-tuple-element.28), channel_id=1, source_target_pairs={{0,12},{4,8},{8,4},{12,0},{1,13},{5,9},{9,5},{13,1},{2,14},{6,10},... | collective-permute-start | bytes 245768 | tf_op jit(solution)/shard_map/ppermute | solution.py:298
  24.3 0.9 %copy-start = (bf16[2,128,256]{2,1,0:T(8,128)(2,1)S(1)}, bf16[2,128,256]{2,1,0:T(8,128)(2,1)}, u32[]{:S(2)}) copy-start(bf16[2,128,256]{2,1,0:T(8,128)(2,1)} %get-tuple-element.18.mw_ref) | copy-start | bytes 393220
  25.2 0.9 %copy-start.1 = (f32[2,16,640]{2,1,0:T(8,128)S(1)}, f32[2,16,640]{2,1,0:T(8,128)}, u32[]{:S(2)}) copy-start(f32[2,16,640]{2,1,0:T(8,128)} %get-tuple-element.19.refs_0_) | copy-start | bytes 245764
  26.1 0.9 %copy-start.2 = (f32[2,16,640]{2,1,0:T(8,128)S(1)}, f32[2,16,640]{2,1,0:T(8,128)}, u32[]{:S(2)}) copy-start(f32[2,16,640]{2,1,0:T(8,128)} %get-tuple-element.25.refs_4_) | copy-start | bytes 245764
  27.0 0.7 %copy-start.3 = (s32[8,128]{1,0:T(8,128)S(1)}, s32[8,128]{1,0:T(8,128)}, u32[]{:S(2)}) copy-start(s32[8,128]{1,0:T(8,128)} %get-tuple-element.17.slot_ref) | copy-start | bytes 12292

commit v2 on v1

--- a/solution.py
+++ b/solution.py
@@ -129,6 +129,7 @@
             pltpu.VMEM((2, nx // LANES, depth + 2 * RIM, LANES), jnp.float32),
             pltpu.VMEM((2, rows, nx + 2 * MAXLAG), jnp.float32),
         ],
+        compiler_params=pltpu.CompilerParams(vmem_limit_bytes=60 << 20),
         name=name,
     )(cell, amp, *halos, *fields)
 
@@ -158,6 +159,7 @@
     return pl.pallas_call(
         weight_body,
         out_shape=[jax.ShapeDtypeStruct((2, na, ROWS), jnp.bfloat16), jax.ShapeDtypeStruct((GROUP, LANES), jnp.int32)],
+        compiler_params=pltpu.CompilerParams(vmem_limit_bytes=60 << 20),
         name="angle_weights",
     )(shifts.reshape(1, -1), angle_map)
 
@@ -203,19 +205,30 @@
         for i in range(MB):
             obuf[pl.ds(8 * (mb * MB + i) + rho, na, stride=PITCH), :] = res[:, i * LANES : (i + 1) * LANES]
 
-    items = [(rho, mb) for rho in range(GROUP) for mb in range(steps)]
-    for i, (rho, mb) in enumerate(items):
-        fill(rho, mb, i % 2)
-        if i:
-            contract(*items[i - 1], (i - 1) % 2)
-    contract(*items[-1], (len(items) - 1) % 2)
-
-
-def image_body(blocks, shots, slot_ref, mw_ref, *refs):
+    def turn(rhos):
+        items = [(rho, mb) for rho in rhos for mb in range(steps)]
+        for i, (rho, mb) in enumerate(items):
+            fill(rho, mb, i % 2)
+            if i:
+                contract(*items[i - 1], (i - 1) % 2)
+        contract(*items[-1], (len(items) - 1) % 2)
+
+    if shots <= 4:
+        turn(range(GROUP))
+    else:
+
+        @pl.loop(0, GROUP)
+        def _(rho):
+            turn([rho])
+
+
+def image_body(blocks, shots, slot_hbm, mw_hbm, *refs):
     sent = refs[: 2 * shots]
-    out_ref, held, fwd, rev, obuf, stage, in_sems, out_sems = refs[2 * shots :]
+    out_ref, slot_ref, mw_ref, held, fwd, rev, obuf, stage, in_sems, out_sems = refs[2 * shots :]
     na, depth, _ = out_ref.shape
     fetches = [pltpu.make_async_copy(sent[i], held.at[i], in_sems.at[i]) for i in range(2 * shots)]
+    fetches.append(pltpu.make_async_copy(slot_hbm, slot_ref, in_sems.at[2 * shots]))
+    fetches.append(pltpu.make_async_copy(mw_hbm, mw_ref, in_sems.at[2 * shots + 1]))
     for fetch in fetches:
         fetch.start()
 
@@ -266,23 +279,24 @@
     full = inner[0].shape[2]
     width = full - 2 * MAXLAG
     na = mw.shape[1]
-    vmem = pl.BlockSpec(memory_space=pltpu.VMEM)
     anywhere = pl.BlockSpec(memory_space=pl.ANY)
     return pl.pallas_call(
         functools.partial(image_body, width // LANES, shots),
         out_shape=jax.ShapeDtypeStruct((na, depth, width), jnp.float32),
-        in_specs=[vmem, vmem] + [anywhere] * (2 * shots),
-        out_specs=anywhere,
+        in_specs=[anywhere] * (2 + 2 * shots),
+        out_specs=pl.BlockSpec(memory_space=pltpu.HBM),
         scratch_shapes=[
+            pltpu.VMEM(slot.shape, slot.dtype),
+            pltpu.VMEM(mw.shape, mw.dtype),
             pltpu.VMEM((2 * shots, *inner[0].shape), jnp.float32),
             pltpu.VMEM((shots, ROWS, LANES), jnp.float32),
             pltpu.VMEM((shots, ROWS, LANES), jnp.float32),
             pltpu.VMEM((na * PITCH, LANES), jnp.float32),
             pltpu.VMEM((na, depth, width), jnp.float32),
-            pltpu.SemaphoreType.DMA((2 * shots,)),
+            pltpu.SemaphoreType.DMA((2 * shots + 2,)),
             pltpu.SemaphoreType.DMA((na // APART,)),
         ],
-        compiler_params=pltpu.CompilerParams(vmem_limit_bytes=40 << 20),
+        compiler_params=pltpu.CompilerParams(vmem_limit_bytes=60 << 20),
         name="angle_image",
     )(slot, mw, *inner, *outer)
 

time: 38.1 us -> 35.8 us (0.940)
  local copies, waits for them, and re-layouts: 3.97 us -> 1.26 us
  Pallas kernels: 17.8 us -> 18.3 us
    unnamed x12 -> x16, local copies, waits for them, and re-layouts: 3.97 us -> 1.26 us
    pallas_call x1, Pallas kernels: 10.1 us -> 10.5 us  [angle_image(): pl.pallas_call(functools.partial(image_body, width // LANES, shots), out_...]
  transfers between devices with their start and end apart: 8 -> 8, of which waited for: 3 -> 3; matrix products, arithmetic and copies ran while one was open for 0% -> 0% of each run, Pallas kernels for 13% -> 14%
where the time goes in v2:
time: 35.8 us; the launch traced here: 35.5 us
  Pallas kernels  18.3 us (51%)
  starting transfers between devices  9.75 us (27%)
  waiting for transfers between devices  6.15 us (17%)
  local copies, waits for them, and re-layouts  1.26 us (4%)
    pallas_call x1, Pallas kernels, angle_image(): pl.pallas_call(functools.partial(image_body, width // LANES, shots), out_...  10.5 us
    pallas_call x2, Pallas kernels, windows(): pl.pallas_call(functools.partial(body, width), in_specs=[smem, smem] + [v...  5.86 us
    ppermute x1, starting transfers between devices, body(): above = lax.ppermute(down, 'space', [(i, i + 1) for i in range(slabs - 1)])  4.46 us
    ppermute x6, starting transfers between devices, exchanged(): lax.ppermute(wins[d], 'offset', [(i, i ^ d) for i in range(count)])  4 us
    ppermute x1, waiting for transfers between devices, body(): below = lax.ppermute(up, 'space', [(i + 1, i) for i in range(slabs - 1)])  3.42 us
    ppermute x6, waiting for transfers between devices, exchanged(): lax.ppermute(wins[d], 'offset', [(i, i ^ d) for i in range(count)])  2.73 us
    pallas_call x1, Pallas kernels, angle_weights(): pl.pallas_call(weight_body, out_shape=[jax.ShapeDtypeStruct((2, na, ROWS)...  1.88 us
    ppermute x1, starting transfers between devices, body(): below = lax.ppermute(up, 'space', [(i + 1, i) for i in range(slabs - 1)])  1.29 us
  transfers between devices with their start and end apart: 8, of which 3 were waited for; matrix products, arithmetic and copies ran while one was open for 0% of the time, Pallas kernels for 14%

profile of v2, /device:TPU:0, one launch (start us, length us, event | category | flops | bytes accessed | tf_op | source)
XLA Modules:
  0.0 35.5 jit_solution(13664348502286128764)
XLA Ops:
  0.0 2.9 %inner_rows.1 = (f32[8,2048]{1,0:T(8,128)}, f32[8,2048]{1,0:T(8,128)}, f32[2,16,640]{2,1,0:T(8,128)}, f32[2,16,640]{2,1,0:T(8,128)}, f32[2,16,640]{2,1,0:T(8,128)}, /*index=5*/f32[2,16,640]{2,1,0:T(8,128)}) custom-call(s32[4]{0:T(128)} %cell_ref.3, f32[4]{0:T(128)} %amp_ref.3, f32[1,32,2048]{2,1,0:T(8,128)} %src_now.3, f32[1,32,2048]{2,1,0:T(8,128)} %src_prev.3, ...), custom_call_target="tpu_custom_call" | custom-call | tf_op jit(solution)/shard_map/inner_rows/pallas_call | solution.py:123
  2.9 0.5 %collective-permute-start = (f32[2,16,640]{2,1,0:T(8,128)}, f32[2,16,640]{2,1,0:T(8,128)S(1)}, u32[]{:S(2)}, u32[]{:S(2)}) collective-permute-start(f32[2,16,640]{2,1,0:T(8,128)} %get-tuple-element.20), channel_id=1, source_target_pairs={{0,4},{4,0},{8,12},{12,8},{1,5},{5,1},{9,13},{13,9},{2,6},{6,2},{1... | collective-permute-start | bytes 245768 | tf_op jit(solution)/shard_map/ppermute | solution.py:312
  3.4 4.5 %collective-permute-start.3 = (f32[8,2048]{1,0:T(8,128)}, f32[8,2048]{1,0:T(8,128)S(1)}, u32[]{:S(2)}, u32[]{:S(2)}) collective-permute-start(f32[8,2048]{1,0:T(8,128)} %get-tuple-element.23), channel_id=1, source_target_pairs={{0,1},{1,2},{2,3},{4,5},{5,6},{6,7},{8,9},{9,10},{10,11},{12,13},{... | collective-permute-start | bytes 196616 | tf_op jit(solution)/shard_map/ppermute | solution.py:318
  7.9 1.3 %collective-permute-start.4 = (f32[8,2048]{1,0:T(8,128)}, f32[8,2048]{1,0:T(8,128)S(1)}, u32[]{:S(2)}, u32[]{:S(2)}) collective-permute-start(f32[8,2048]{1,0:T(8,128)} %get-tuple-element.24), channel_id=1, source_target_pairs={{1,0},{2,1},{3,2},{5,4},{6,5},{7,6},{9,8},{10,9},{11,10},{13,12},{... | collective-permute-start | bytes 196616 | tf_op jit(solution)/shard_map/ppermute | solution.py:317
  9.2 1.6 %collective-permute-start.1 = (f32[2,16,640]{2,1,0:T(8,128)}, f32[2,16,640]{2,1,0:T(8,128)S(1)}, u32[]{:S(2)}, u32[]{:S(2)}) collective-permute-start(f32[2,16,640]{2,1,0:T(8,128)} %get-tuple-element.21), channel_id=1, source_target_pairs={{0,8},{4,12},{8,0},{12,4},{1,9},{5,13},{9,1},{13,5},{2,10},{6,14},... | collective-permute-start | bytes 245768 | tf_op jit(solution)/shard_map/ppermute | solution.py:312
  10.7 0.1 collective-permute-start.2
  10.8 0.0 collective-permute-done.3.above
  10.8 0.0 copy-start.6
  10.8 3.4 %collective-permute-done.4.below = f32[8,2048]{1,0:T(8,128)S(1)} collective-permute-done((f32[8,2048]{1,0:T(8,128)}, f32[8,2048]{1,0:T(8,128)S(1)}, u32[]{:S(2)}, u32[]{:S(2)}) %collective-permute-start.4) | collective-permute-done | bytes 65568 | tf_op jit(solution)/shard_map/ppermute | solution.py:317
  14.2 0.0 copy-done.6
  14.2 0.0 copy-start.7
  14.2 0.6 %copy-done.7 = f32[8,2048]{1,0:T(8,128)} copy-done((f32[8,2048]{1,0:T(8,128)}, f32[8,2048]{1,0:T(8,128)S(1)}, u32[]{:S(2)}) %copy-start.7) | copy-done | bytes 65560
  14.9 3.0 %outer_rows.1 = (f32[2,16,640]{2,1,0:T(8,128)}, f32[2,16,640]{2,1,0:T(8,128)}, f32[2,16,640]{2,1,0:T(8,128)}, f32[2,16,640]{2,1,0:T(8,128)}) custom-call(s32[4]{0:T(128)} %cell_ref.3, f32[4]{0:T(128)} %amp_ref.3, f32[8,2048]{1,0:T(8,128)} %copy-done.6, f32[8,2048]{1,0:T(8,128)} %copy-done.7, f32[1,32,2048]{2,1,0:T(8,128)} %src_now.3, ...), custom_call_target="tpu_custom_call" | custom-call | tf_op jit(solution)/shard_map/outer_rows/pallas_call | solution.py:123
  17.8 0.0 collective-permute-start.5
  17.8 1.5 %collective-permute-start.6 = (f32[2,16,640]{2,1,0:T(8,128)}, f32[2,16,640]{2,1,0:T(8,128)S(1)}, u32[]{:S(2)}, u32[]{:S(2)}) collective-permute-start(f32[2,16,640]{2,1,0:T(8,128)} %get-tuple-element.27), channel_id=1, source_target_pairs={{0,8},{4,12},{8,0},{12,4},{1,9},{5,13},{9,1},{13,5},{2,10},{6,14},... | collective-permute-start | bytes 245768 | tf_op jit(solution)/shard_map/ppermute | solution.py:312
  19.4 0.0 collective-permute-done.refs_1_
  19.4 0.0 copy-start
  19.4 0.3 collective-permute-start.7
  19.7 1.9 %angle_weights.1 = (bf16[2,128,256]{2,1,0:T(8,128)(2,1)}, s32[8,128]{1,0:T(8,128)}) custom-call(s32[1,128]{1,0:T(1,128)} %bitcast.1, f32[128,128]{1,0:T(8,128)} %map_ref.1), custom_call_target="tpu_custom_call" | custom-call | tf_op jit(solution)/shard_map/angle_weights/pallas_call | solution.py:159
  21.6 0.0 collective-permute-done.1.refs_2_
  21.6 0.0 copy-start.1
  21.6 0.0 collective-permute-done.2.refs_3_
  21.6 0.0 copy-start.2
  21.6 0.0 collective-permute-done.5.refs_5_
  21.6 0.0 copy-start.3
  21.6 1.6 %collective-permute-done.6.refs_6_ = f32[2,16,640]{2,1,0:T(8,128)S(1)} collective-permute-done((f32[2,16,640]{2,1,0:T(8,128)}, f32[2,16,640]{2,1,0:T(8,128)S(1)}, u32[]{:S(2)}, u32[]{:S(2)}) %collective-permute-start.6) | collective-permute-done | bytes 81952 | tf_op jit(solution)/shard_map/ppermute | solution.py:312
  23.2 0.0 copy-start.4
  23.2 1.1 %collective-permute-done.7.refs_7_ = f32[2,16,640]{2,1,0:T(8,128)S(1)} collective-permute-done((f32[2,16,640]{2,1,0:T(8,128)}, f32[2,16,640]{2,1,0:T(8,128)S(1)}, u32[]{:S(2)}, u32[]{:S(2)}) %collective-permute-start.7) | collective-permute-done | bytes 81952 | tf_op jit(solution)/shard_map/ppermute | solution.py:312
  24.3 0.0 copy-start.5
  24.3 0.0 copy-done
  24.3 0.0 copy-done.1
  24.3 0.0 copy-done.2
  24.3 0.0 copy-done.3
  24.4 0.0 copy-done.4
  24.4 0.6 %copy-done.5 = f32[2,16,640]{2,1,0:T(8,128)} copy-done((f32[2,16,640]{2,1,0:T(8,128)}, f32[2,16,640]{2,1,0:T(8,128)S(1)}, u32[]{:S(2)}) %copy-start.5) | copy-done | bytes 81944
  25.0 10.5 %angle_image.1 = f32[128,32,512]{2,1,0:T(8,128)} custom-call(s32[8,128]{1,0:T(8,128)} %get-tuple-element.17.slot_hbm, bf16[2,128,256]{2,1,0:T(8,128)(2,1)} %get-tuple-element.18.mw_hbm, f32[2,16,640]{2,1,0:T(8,128)} %get-tuple-element.19.refs_0_, f32[2,16,640]{2,1,0:T(8,128)} %copy-done, f32[2,16,640]{2,1,0:T(8,128)} %copy-done.1, f32[2,16,640]{2,1,0:T(8,128)} %copy-done.2, ...), custom_call_target="tpu_custom_call" | custom-call | tf_op jit(solution)/shard_map/angle_image/pallas_call | solution.py:283
Async XLA Ops:
  2.9 16.5 %collective-permute-start = (f32[2,16,640]{2,1,0:T(8,128)}, f32[2,16,640]{2,1,0:T(8,128)S(1)}, u32[]{:S(2)}, u32[]{:S(2)}) collective-permute-start(f32[2,16,640]{2,1,0:T(8,128)} %get-tuple-element.20), channel_id=1, source_target_pairs={{0,4},{4,0},{8,12},{12,8},{1,5},{5,1},{9,13},{13,9},{2,6},{6,2},{1... | collective-permute-start | bytes 245768 | tf_op jit(solution)/shard_map/ppermute | solution.py:312
  3.4 7.4 %collective-permute-start.3 = (f32[8,2048]{1,0:T(8,128)}, f32[8,2048]{1,0:T(8,128)S(1)}, u32[]{:S(2)}, u32[]{:S(2)}) collective-permute-start(f32[8,2048]{1,0:T(8,128)} %get-tuple-element.23), channel_id=1, source_target_pairs={{0,1},{1,2},{2,3},{4,5},{5,6},{6,7},{8,9},{9,10},{10,11},{12,13},{... | collective-permute-start | bytes 196616 | tf_op jit(solution)/shard_map/ppermute | solution.py:318
  7.9 6.4 %collective-permute-start.4 = (f32[8,2048]{1,0:T(8,128)}, f32[8,2048]{1,0:T(8,128)S(1)}, u32[]{:S(2)}, u32[]{:S(2)}) collective-permute-start(f32[8,2048]{1,0:T(8,128)} %get-tuple-element.24), channel_id=1, source_target_pairs={{1,0},{2,1},{3,2},{5,4},{6,5},{7,6},{9,8},{10,9},{11,10},{13,12},{... | collective-permute-start | bytes 196616 | tf_op jit(solution)/shard_map/ppermute | solution.py:317
  9.2 12.4 %collective-permute-start.1 = (f32[2,16,640]{2,1,0:T(8,128)}, f32[2,16,640]{2,1,0:T(8,128)S(1)}, u32[]{:S(2)}, u32[]{:S(2)}) collective-permute-start(f32[2,16,640]{2,1,0:T(8,128)} %get-tuple-element.21), channel_id=1, source_target_pairs={{0,8},{4,12},{8,0},{12,4},{1,9},{5,13},{9,1},{13,5},{2,10},{6,14},... | collective-permute-start | bytes 245768 | tf_op jit(solution)/shard_map/ppermute | solution.py:312
  10.7 10.9 %collective-permute-start.2 = (f32[2,16,640]{2,1,0:T(8,128)}, f32[2,16,640]{2,1,0:T(8,128)S(1)}, u32[]{:S(2)}, u32[]{:S(2)}) collective-permute-start(f32[2,16,640]{2,1,0:T(8,128)} %get-tuple-element.22), channel_id=1, source_target_pairs={{0,12},{4,8},{8,4},{12,0},{1,13},{5,9},{9,5},{13,1},{2,14},{6,10},... | collective-permute-start | bytes 245768 | tf_op jit(solution)/shard_map/ppermute | solution.py:312
  10.8 3.4 %copy-start.6 = (f32[8,2048]{1,0:T(8,128)}, f32[8,2048]{1,0:T(8,128)S(1)}, u32[]{:S(2)}) copy-start(f32[8,2048]{1,0:T(8,128)S(1)} %collective-permute-done.3.above) | copy-start | bytes 196612
  14.2 0.6 %copy-start.7 = (f32[8,2048]{1,0:T(8,128)}, f32[8,2048]{1,0:T(8,128)S(1)}, u32[]{:S(2)}) copy-start(f32[8,2048]{1,0:T(8,128)S(1)} %collective-permute-done.4.below) | copy-start | bytes 196612
  17.8 3.8 %collective-permute-start.5 = (f32[2,16,640]{2,1,0:T(8,128)}, f32[2,16,640]{2,1,0:T(8,128)S(1)}, u32[]{:S(2)}, u32[]{:S(2)}) collective-permute-start(f32[2,16,640]{2,1,0:T(8,128)} %get-tuple-element.26), channel_id=1, source_target_pairs={{0,4},{4,0},{8,12},{12,8},{1,5},{5,1},{9,13},{13,9},{2,6},{6,2},{1... | collective-permute-start | bytes 245768 | tf_op jit(solution)/shard_map/ppermute | solution.py:312
  17.8 5.4 %collective-permute-start.6 = (f32[2,16,640]{2,1,0:T(8,128)}, f32[2,16,640]{2,1,0:T(8,128)S(1)}, u32[]{:S(2)}, u32[]{:S(2)}) collective-permute-start(f32[2,16,640]{2,1,0:T(8,128)} %get-tuple-element.27), channel_id=1, source_target_pairs={{0,8},{4,12},{8,0},{12,4},{1,9},{5,13},{9,1},{13,5},{2,10},{6,14},... | collective-permute-start | bytes 245768 | tf_op jit(solution)/shard_map/ppermute | solution.py:312
  19.4 5.0 %copy-start = (f32[2,16,640]{2,1,0:T(8,128)}, f32[2,16,640]{2,1,0:T(8,128)S(1)}, u32[]{:S(2)}) copy-start(f32[2,16,640]{2,1,0:T(8,128)S(1)} %collective-permute-done.refs_1_) | copy-start | bytes 245764
  19.4 5.0 %collective-permute-start.7 = (f32[2,16,640]{2,1,0:T(8,128)}, f32[2,16,640]{2,1,0:T(8,128)S(1)}, u32[]{:S(2)}, u32[]{:S(2)}) collective-permute-start(f32[2,16,640]{2,1,0:T(8,128)} %get-tuple-element.28), channel_id=1, source_target_pairs={{0,12},{4,8},{8,4},{12,0},{1,13},{5,9},{9,5},{13,1},{2,14},{6,10},... | collective-permute-start | bytes 245768 | tf_op jit(solution)/shard_map/ppermute | solution.py:312
  21.6 2.8 %copy-start.1 = (f32[2,16,640]{2,1,0:T(8,128)}, f32[2,16,640]{2,1,0:T(8,128)S(1)}, u32[]{:S(2)}) copy-start(f32[2,16,640]{2,1,0:T(8,128)S(1)} %collective-permute-done.1.refs_2_) | copy-start | bytes 245764
  21.6 2.8 %copy-start.2 = (f32[2,16,640]{2,1,0:T(8,128)}, f32[2,16,640]{2,1,0:T(8,128)S(1)}, u32[]{:S(2)}) copy-start(f32[2,16,640]{2,1,0:T(8,128)S(1)} %collective-permute-done.2.refs_3_) | copy-start | bytes 245764
  21.6 2.7 %copy-start.3 = (f32[2,16,640]{2,1,0:T(8,128)}, f32[2,16,640]{2,1,0:T(8,128)S(1)}, u32[]{:S(2)}) copy-start(f32[2,16,640]{2,1,0:T(8,128)S(1)} %collective-permute-done.5.refs_5_) | copy-start | bytes 245764
  23.2 1.1 %copy-start.4 = (f32[2,16,640]{2,1,0:T(8,128)}, f32[2,16,640]{2,1,0:T(8,128)S(1)}, u32[]{:S(2)}) copy-start(f32[2,16,640]{2,1,0:T(8,128)S(1)} %collective-permute-done.6.refs_6_) | copy-start | bytes 245764
  24.3 0.6 %copy-start.5 = (f32[2,16,640]{2,1,0:T(8,128)}, f32[2,16,640]{2,1,0:T(8,128)S(1)}, u32[]{:S(2)}) copy-start(f32[2,16,640]{2,1,0:T(8,128)S(1)} %collective-permute-done.7.refs_7_) | copy-start | bytes 245764

commit v3 on v2

--- a/solution.py
+++ b/solution.py
@@ -40,11 +40,11 @@
     return total
 
 
-def step_rows(jobs, width, cell_ref, amp_ref, prevs, courant, rows_ref, padded, outs):
-    pitch = rows_ref.shape[2]
-    count = len(outs)
-    nx = courant.shape[1]
-    depth = courant.shape[0]
+def step_body(width, cell_ref, amp_ref, src_now, src_prev, rcv_now, rcv_prev, courant, speed_ref, *refs):
+    count = (len(refs) - 4) // 2
+    rims, wins = refs[:count], refs[count : 2 * count]
+    rows_ref, padded, padded_rim, padded_speed = refs[2 * count :]
+    depth, nx = src_now.shape[1:]
     blocks = nx // LANES
     me = lax.axis_index("offset")
     cell = cell_ref[me] - lax.axis_index("space") * depth * nx
@@ -56,82 +56,94 @@
     mirror = (lax.rem(source + target + 1, LANES) == MAXLAG).astype(jnp.float32)
     half = lane < MAXLAG
     zero = jnp.zeros((GROUP, LANES), jnp.float32)
+
+    def place(ref, f, row, out):
+        if f == 0:
+            turned = jnp.dot(
+                jnp.concatenate(out[::-1], 0), mirror, precision=lax.Precision.HIGHEST, preferred_element_type=jnp.float32
+            )
+            out = [turned[t * GROUP : (t + 1) * GROUP, :] for t in range(blocks)]
+        else:
+            out = [pltpu.roll(v, MAXLAG, 1) for v in out]
+        out = [zero] + out + [zero]
+        for t in range(blocks + 1):
+            ref[f, row : row + GROUP, t * LANES : (t + 1) * LANES] = jnp.where(half, out[t], out[t + 1])
+
+    cuts = [slice(t * LANES, (t + 1) * LANES) for t in range(blocks)]
+    nows, prevs = (src_now, rcv_now), (src_prev, rcv_prev)
     for f in range(2):
-        for row, z in jobs:
-            tiles = [rows_ref[f, t, z + RIM : z + RIM + GROUP, :] for t in range(blocks)]
+        now = nows[f]
+        place(padded_rim, f, 0, [jnp.concatenate([now[0, :RIM, at], now[0, depth - RIM :, at]], 0) for at in cuts])
+        for b, z in enumerate((0, depth - GROUP)):
+            place(padded_speed, f, b * GROUP, [courant[z : z + GROUP, at] for at in cuts])
+        for t in range(blocks):
+            rows_ref[f, t, 0:GROUP, :] = zero
+            rows_ref[f, t, GROUP : GROUP + depth, :] = now[0, :, cuts[t]]
+            rows_ref[f, t, GROUP + depth : 2 * GROUP + depth, :] = zero
+        for z in range(0, depth, GROUP):
+            at = z + GROUP
+            tiles = [rows_ref[f, t, at : at + GROUP, :] for t in range(blocks)]
             across = lateral(tiles, lane)
             out = []
             for t in range(blocks):
-                at = slice(t * LANES, (t + 1) * LANES)
                 total = (2.0 * coeffs[0]) * tiles[t] + across[t]
                 for k in range(1, RIM + 1):
-                    total = total + coeffs[k] * (
-                        rows_ref[f, t, z + RIM - k : z + RIM - k + GROUP, :] + rows_ref[f, t, z + RIM + k : z + RIM + k + GROUP, :]
-                    )
-                value = 2.0 * tiles[t] - prevs[f][0, z : z + GROUP, at] + courant[z : z + GROUP, at] * total
+                    total = total + coeffs[k] * (rows_ref[f, t, at - k : at - k + GROUP, :] + rows_ref[f, t, at + k : at + k + GROUP, :])
+                value = 2.0 * tiles[t] - prevs[f][0, z : z + GROUP, cuts[t]] + courant[z : z + GROUP, cuts[t]] * total
                 if f == 0:
                     value = value + jnp.where(flat == cell - (z * nx + t * LANES), amp, 0.0)
                 out.append(value)
-            if f == 0:
-                turned = jnp.dot(
-                    jnp.concatenate(out[::-1], 0), mirror, precision=lax.Precision.HIGHEST, preferred_element_type=jnp.float32
-                )
-                out = [turned[t * GROUP : (t + 1) * GROUP, :] for t in range(blocks)]
-            else:
-                out = [pltpu.roll(v, MAXLAG, 1) for v in out]
-            out = [zero] + out + [zero]
-            for t in range(blocks + 1):
-                padded[f, row : row + GROUP, t * LANES : (t + 1) * LANES] = jnp.where(half, out[t], out[t + 1])
-    for d, out in enumerate(outs):
+            place(padded, f, z, out)
+    for d in range(count):
         other = lax.bitwise_xor(me, d)
         for f, first in enumerate((count - 1 - other, other)):
-            out[f] = padded[f, :, pl.ds(pl.multiple_of(first * width, LANES), width + 2 * MAXLAG)]
-
-
-def inner_body(width, cell_ref, amp_ref, src_now, src_prev, rcv_now, rcv_prev, courant, up_ref, down_ref, *refs):
-    outs, rows_ref, padded = refs[:-2], refs[-2], refs[-1]
-    depth, nx = src_now.shape[1:]
-    for f, now in enumerate((src_now, rcv_now)):
-        up_ref[f * RIM : (f + 1) * RIM, :] = now[0, 0:RIM, :]
-        down_ref[f * RIM : (f + 1) * RIM, :] = now[0, depth - RIM : depth, :]
-        for t in range(nx // LANES):
-            rows_ref[f, t, RIM : RIM + depth, :] = now[0, :, t * LANES : (t + 1) * LANES]
-    jobs = [(z - GROUP, z) for z in range(GROUP, depth - GROUP, GROUP)]
-    step_rows(jobs, width, cell_ref, amp_ref, (src_prev, rcv_prev), courant, rows_ref, padded, outs)
-
-
-def outer_body(width, cell_ref, amp_ref, above, below, src_now, src_prev, rcv_now, rcv_prev, courant, *refs):
-    outs, rows_ref, padded = refs[:-2], refs[-2], refs[-1]
-    depth, nx = src_now.shape[1:]
-    for f, now in enumerate((src_now, rcv_now)):
-        for t in range(nx // LANES):
-            at = slice(t * LANES, (t + 1) * LANES)
-            rows_ref[f, t, 0:RIM, :] = above[f * RIM : (f + 1) * RIM, at]
-            rows_ref[f, t, RIM : RIM + 2 * GROUP, :] = now[0, 0 : 2 * GROUP, at]
-            rows_ref[f, t, RIM + depth - 2 * GROUP : RIM + depth, :] = now[0, depth - 2 * GROUP : depth, at]
-            rows_ref[f, t, RIM + depth : 2 * RIM + depth, :] = below[f * RIM : (f + 1) * RIM, at]
-    jobs = [(0, 0), (GROUP, depth - GROUP)]
-    step_rows(jobs, width, cell_ref, amp_ref, (src_prev, rcv_prev), courant, rows_ref, padded, outs)
-
-
-def windows(body, name, count, rows, halos, extra, cell, amp, fields):
+            at = pl.ds(pl.multiple_of(first * width, LANES), width + 2 * MAXLAG)
+            rims[d][f] = padded_rim[f, :, at]
+            wins[d][f] = padded[f, :, at]
+            if d == 0:
+                speed_ref[f] = padded_speed[f, :, at]
+
+
+def stepped_windows(count, cell, amp, fields):
     depth, nx = fields[0].shape[1:]
     width = nx // count
-    out = jax.ShapeDtypeStruct((2, rows, width + 2 * MAXLAG), jnp.float32)
+    shape = lambda rows: jax.ShapeDtypeStruct((2, rows, width + 2 * MAXLAG), jnp.float32)
     smem = pl.BlockSpec(memory_space=pltpu.SMEM)
     vmem = pl.BlockSpec(memory_space=pltpu.VMEM)
-    return pl.pallas_call(
-        functools.partial(body, width),
-        in_specs=[smem, smem] + [vmem] * (len(halos) + len(fields)),
-        out_specs=[vmem] * (len(extra) + count),
-        out_shape=extra + [out] * count,
+    speed, *rest = pl.pallas_call(
+        functools.partial(step_body, width),
+        in_specs=[smem, smem] + [vmem] * len(fields),
+        out_specs=[vmem] * (1 + 2 * count),
+        out_shape=[shape(2 * GROUP)] + [shape(GROUP)] * count + [shape(depth)] * count,
         scratch_shapes=[
-            pltpu.VMEM((2, nx // LANES, depth + 2 * RIM, LANES), jnp.float32),
-            pltpu.VMEM((2, rows, nx + 2 * MAXLAG), jnp.float32),
+            pltpu.VMEM((2, nx // LANES, depth + 2 * GROUP, LANES), jnp.float32),
+            pltpu.VMEM((2, depth, nx + 2 * MAXLAG), jnp.float32),
+            pltpu.VMEM((2, GROUP, nx + 2 * MAXLAG), jnp.float32),
+            pltpu.VMEM((2, 2 * GROUP, nx + 2 * MAXLAG), jnp.float32),
         ],
         compiler_params=pltpu.CompilerParams(vmem_limit_bytes=60 << 20),
-        name=name,
-    )(cell, amp, *halos, *fields)
+        name="step",
+    )(cell, amp, *fields)
+    return speed, rest[:count], rest[count:]
+
+
+def rim_body(*refs):
+    shots = len(refs) - 2
+    up_ref, down_ref = refs[shots:]
+    for s in range(shots):
+        for f in range(2):
+            up_ref[s, f * RIM : (f + 1) * RIM, :] = refs[s][f, :RIM, :]
+            down_ref[s, f * RIM : (f + 1) * RIM, :] = refs[s][f, RIM:, :]
+
+
+def rims_by_side(rims):
+    out = jax.ShapeDtypeStruct((len(rims), 2 * RIM, rims[0].shape[2]), jnp.float32)
+    return pl.pallas_call(
+        rim_body,
+        out_shape=[out, out],
+        compiler_params=pltpu.CompilerParams(vmem_limit_bytes=60 << 20),
+        name="rims_by_side",
+    )(*rims)
 
 
 def weight_body(shift_ref, map_ref, mw_ref, slot_ref):
@@ -222,29 +234,47 @@
             turn([rho])
 
 
-def image_body(blocks, shots, slot_hbm, mw_hbm, *refs):
-    sent = refs[: 2 * shots]
-    out_ref, slot_ref, mw_ref, held, fwd, rev, obuf, stage, in_sems, out_sems = refs[2 * shots :]
+def image_body(blocks, shots, *refs):
+    given, out_ref = refs[: 5 + shots], refs[5 + shots]
+    slot_ref, mw_ref, speed, above, below, held, ext, fwd, rev, obuf, stage, in_sems, out_sems = refs[6 + shots :]
     na, depth, _ = out_ref.shape
-    fetches = [pltpu.make_async_copy(sent[i], held.at[i], in_sems.at[i]) for i in range(2 * shots)]
-    fetches.append(pltpu.make_async_copy(slot_hbm, slot_ref, in_sems.at[2 * shots]))
-    fetches.append(pltpu.make_async_copy(mw_hbm, mw_ref, in_sems.at[2 * shots + 1]))
+    kept = [slot_ref, mw_ref, speed, above, below] + [held.at[s] for s in range(shots)]
+    fetches = [pltpu.make_async_copy(x, y, in_sems.at[i]) for i, (x, y) in enumerate(zip(given, kept))]
     for fetch in fetches:
         fetch.start()
+    for fetch in fetches:
+        fetch.wait()
+
+    zero = jnp.zeros((GROUP, LANES), jnp.float32)
+    low = depth - GROUP
+    for s in range(shots):
+        for f in range(2):
+            rim = slice(f * RIM, (f + 1) * RIM)
+            for t in range(blocks + 1):
+                at = slice(t * LANES, (t + 1) * LANES)
+                ext[s, f, t, 0:GROUP, :] = zero
+                ext[s, f, t, GROUP : 2 * GROUP, :] = zero
+                ext[s, f, t, 2 * GROUP : 3 * GROUP, :] = zero
+                ext[s, f, t, 3 * GROUP : 4 * GROUP, :] = zero
+                ext[s, f, t, GROUP - RIM : GROUP, :] = above[s, rim, at]
+                ext[s, f, t, 3 * GROUP : 3 * GROUP + RIM, :] = below[s, rim, at]
+                top, bottom = None, None
+                for k in range(1, RIM + 1):
+                    u = coeffs[k] * ext[s, f, t, GROUP - k : 2 * GROUP - k, :]
+                    v = coeffs[k] * ext[s, f, t, 2 * GROUP + k : 3 * GROUP + k, :]
+                    top, bottom = (u, v) if top is None else (top + u, bottom + v)
+                held[s, f, 0:GROUP, at] += speed[f, 0:GROUP, at] * top
+                held[s, f, low:depth, at] += speed[f, GROUP:, at] * bottom
 
     def gathered(s, f, b):
-        inner, outer = held.at[s], held.at[shots + s]
         tiles = []
         for q in range(blocks):
             t = q + b if f else blocks - 1 - q + b
-            at = slice(t * LANES, (t + 1) * LANES)
-            tiles += [outer[f, :GROUP, at], inner[f, :, at], outer[f, GROUP:, at]]
+            tiles.append(held[s, f, :, t * LANES : (t + 1) * LANES])
         if blocks * depth < LANES:
             tiles.append(jnp.zeros((LANES - blocks * depth, LANES), jnp.float32))
         return jnp.concatenate(tiles, 0)
 
-    for fetch in fetches:
-        fetch.wait()
     for s in range(shots):
         for b in range(2):
             fwd[s, b * LANES : (b + 1) * LANES, :] = gathered(s, 1, b).T
@@ -274,52 +304,57 @@
         leave(i).wait()
 
 
-def angle_image(inner, outer, mw, slot, depth):
-    shots = len(inner)
-    full = inner[0].shape[2]
+def angle_image(wins, above, below, speed, mw, slot, depth):
+    shots = len(wins)
+    full = wins[0].shape[2]
     width = full - 2 * MAXLAG
     na = mw.shape[1]
     anywhere = pl.BlockSpec(memory_space=pl.ANY)
+    like = lambda x: pltpu.VMEM(x.shape, x.dtype)
     return pl.pallas_call(
         functools.partial(image_body, width // LANES, shots),
         out_shape=jax.ShapeDtypeStruct((na, depth, width), jnp.float32),
-        in_specs=[anywhere] * (2 + 2 * shots),
+        in_specs=[anywhere] * (5 + shots),
         out_specs=pl.BlockSpec(memory_space=pltpu.HBM),
         scratch_shapes=[
-            pltpu.VMEM(slot.shape, slot.dtype),
-            pltpu.VMEM(mw.shape, mw.dtype),
-            pltpu.VMEM((2 * shots, *inner[0].shape), jnp.float32),
+            like(slot),
+            like(mw),
+            like(speed),
+            like(above),
+            like(below),
+            pltpu.VMEM((shots, *wins[0].shape), jnp.float32),
+            pltpu.VMEM((shots, 2, full // LANES, 4 * GROUP, LANES), jnp.float32),
             pltpu.VMEM((shots, ROWS, LANES), jnp.float32),
             pltpu.VMEM((shots, ROWS, LANES), jnp.float32),
             pltpu.VMEM((na * PITCH, LANES), jnp.float32),
             pltpu.VMEM((na, depth, width), jnp.float32),
-            pltpu.SemaphoreType.DMA((2 * shots + 2,)),
+            pltpu.SemaphoreType.DMA((5 + shots,)),
             pltpu.SemaphoreType.DMA((na // APART,)),
         ],
         compiler_params=pltpu.CompilerParams(vmem_limit_bytes=60 << 20),
         name="angle_image",
-    )(slot, mw, *inner, *outer)
+    )(slot, mw, speed, above, below, *wins)
 
 
 def body(src_now, src_prev, rcv_now, rcv_prev, courant, shot_cell, wavelet, shifts, angle_map):
     depth = src_now.shape[1]
     count = lax.axis_size("offset")
     slabs = lax.axis_size("space")
-    fields = (src_now, src_prev, rcv_now, rcv_prev, courant)
-    edge = jax.ShapeDtypeStruct((2 * RIM, src_now.shape[2]), jnp.float32)
-
-    def exchanged(wins):
-        return [wins[0]] + [lax.ppermute(wins[d], "offset", [(i, i ^ d) for i in range(count)]) for d in range(1, count)]
-
-    up, down, *inner = windows(
-        inner_body, "inner_rows", count, depth - 2 * GROUP, (), [edge, edge], shot_cell, wavelet, fields
-    )
+
+    def exchanged(parts):
+        out = [parts[0]]
+        for d in range(1, count):
+            out.append(lax.ppermute(parts[d], "offset", [(i, i ^ d) for i in range(count)]))
+        return out
+
+    speed, rims, wins = stepped_windows(count, shot_cell, wavelet, (src_now, src_prev, rcv_now, rcv_prev, courant))
+    rims = exchanged(rims)
+    wins = exchanged(wins)
+    up, down = rims_by_side(rims)
     below = lax.ppermute(up, "space", [(i + 1, i) for i in range(slabs - 1)])
     above = lax.ppermute(down, "space", [(i, i + 1) for i in range(slabs - 1)])
-    inner = exchanged(inner)
-    outer = exchanged(windows(outer_body, "outer_rows", count, 2 * GROUP, (above, below), [], shot_cell, wavelet, fields))
     mw, slot = angle_weights(shifts, angle_map)
-    return angle_image(inner, outer, mw, slot, depth)
+    return angle_image(wins, above, below, speed, mw, slot, depth)
 
 
 def solution(mesh):

time: 35.8 us -> 41.1 us (1.15)
  waiting for transfers between devices: 6.15 us -> 11 us
  starting transfers between devices: 9.75 us -> 10.3 us
    ppermute x6, waiting for transfers between devices: 2.73 us -> 7.65 us  [exchanged(): lax.ppermute(parts[d], 'offset', [(i, i ^ d) for i in range(count)])]
    ppermute x6, starting transfers between devices: 4 us -> 5.3 us  [exchanged(): lax.ppermute(parts[d], 'offset', [(i, i ^ d) for i in range(count)])]
    ppermute x1, starting transfers between devices: 4.46 us -> 3.72 us  [body(): above = lax.ppermute(down, 'space', [(i, i + 1) for i in range(slabs - 1)])]
  transfers between devices with their start and end apart: 8 -> 8, of which waited for: 3 -> 2; matrix products, arithmetic and copies ran while one was open for 0% -> 0% of each run, Pallas kernels for 14% -> 8%
where the time goes in v3:
time: 41.1 us; the launch traced here: 40.8 us
  Pallas kernels  18 us (44%)
  waiting for transfers between devices  11 us (27%)
  starting transfers between devices  10.3 us (25%)
  local copies, waits for them, and re-layouts  1.41 us (3%)
    pallas_call x1, Pallas kernels, angle_image(): pl.pallas_call(functools.partial(image_body, width // LANES, shots), out_...  10.7 us
    ppermute x6, waiting for transfers between devices, exchanged(): lax.ppermute(parts[d], 'offset', [(i, i ^ d) for i in range(count)])  7.65 us
    ppermute x6, starting transfers between devices, exchanged(): lax.ppermute(parts[d], 'offset', [(i, i ^ d) for i in range(count)])  5.3 us
    pallas_call x1, Pallas kernels, stepped_windows(): pl.pallas_call(functools.partial(step_body, width), in_specs=[smem, smem]...  3.94 us
    ppermute x1, starting transfers between devices, body(): above = lax.ppermute(down, 'space', [(i, i + 1) for i in range(slabs - 1)])  3.72 us
    ppermute x1, waiting for transfers between devices, body(): below = lax.ppermute(up, 'space', [(i + 1, i) for i in range(slabs - 1)])  3.36 us
    pallas_call x1, Pallas kernels, angle_weights(): pl.pallas_call(weight_body, out_shape=[jax.ShapeDtypeStruct((2, na, ROWS)...  1.88 us
    pallas_call x1, Pallas kernels, rims_by_side(): pl.pallas_call(rim_body, out_shape=[out, out], compiler_params=pltpu.Comp...  1.54 us
  transfers between devices with their start and end apart: 8, of which 2 were waited for; matrix products, arithmetic and copies ran while one was open for 0% of the time, Pallas kernels for 8%

profile of v3, /device:TPU:0, one launch (start us, length us, event | category | flops | bytes accessed | tf_op | source)
XLA Modules:
  0.0 40.8 jit_solution(4791872516412078288)
XLA Ops:
  0.0 3.9 %step.1 = (f32[2,16,640]{2,1,0:T(8,128)}, f32[2,8,640]{2,1,0:T(8,128)}, f32[2,8,640]{2,1,0:T(8,128)}, f32[2,8,640]{2,1,0:T(8,128)}, f32[2,8,640]{2,1,0:T(8,128)}...) custom-call(s32[4]{0:T(128)} %cell_ref.1, f32[4]{0:T(128)} %amp_ref.1, ...), custom_call_target="tpu_custom_call" | custom-call | tf_op jit(solution)/shard_map/step/pallas_call | solution.py:113
  3.9 0.5 %collective-permute-start = (f32[2,8,640]{2,1,0:T(8,128)}, f32[2,8,640]{2,1,0:T(8,128)S(1)}, u32[]{:S(2)}, u32[]{:S(2)}) collective-permute-start(f32[2,8,640]{2,1,0:T(8,128)} %get-tuple-element.22), channel_id=1, source_target_pairs={{0,4},{4,0},{8,12},{12,8},{1,5},{5,1},{9,13},{13,9},{2,6},{6,2},{1... | collective-permute-start | bytes 122888 | tf_op jit(solution)/shard_map/ppermute | solution.py:347
  4.4 0.1 collective-permute-start.5
  4.5 2.9 %collective-permute-start.6 = (f32[2,32,640]{2,1,0:T(8,128)}, f32[2,32,640]{2,1,0:T(8,128)S(1)}, u32[]{:S(2)}, u32[]{:S(2)}) collective-permute-start(f32[2,32,640]{2,1,0:T(8,128)} %get-tuple-element.29), channel_id=1, source_target_pairs={{0,8},{4,12},{8,0},{12,4},{1,9},{5,13},{9,1},{13,5},{2,10},{6,14},... | collective-permute-start | bytes 491528 | tf_op jit(solution)/shard_map/ppermute | solution.py:347
  7.4 0.0 collective-permute-start.7
  7.4 1.4 %collective-permute-start.1 = (f32[2,8,640]{2,1,0:T(8,128)}, f32[2,8,640]{2,1,0:T(8,128)S(1)}, u32[]{:S(2)}, u32[]{:S(2)}) collective-permute-start(f32[2,8,640]{2,1,0:T(8,128)} %get-tuple-element.23), channel_id=1, source_target_pairs={{0,8},{4,12},{8,0},{12,4},{1,9},{5,13},{9,1},{13,5},{2,10},{6,14},... | collective-permute-start | bytes 122888 | tf_op jit(solution)/shard_map/ppermute | solution.py:347
  8.8 0.0 collective-permute-done.refs_1_
  8.8 0.0 copy-start.5
  8.8 0.4 collective-permute-start.2
  9.2 7.6 %collective-permute-done.1.refs_2_ = f32[2,8,640]{2,1,0:T(8,128)S(1)} collective-permute-done((f32[2,8,640]{2,1,0:T(8,128)}, f32[2,8,640]{2,1,0:T(8,128)S(1)}, u32[]{:S(2)}, u32[]{:S(2)}) %collective-permute-start.1) | collective-permute-done | bytes 40992 | tf_op jit(solution)/shard_map/ppermute | solution.py:347
  16.9 0.0 copy-start.6
  16.9 0.0 collective-permute-done.2.refs_3_
  16.9 0.0 copy-start.7
  16.9 0.0 copy-done.5
  16.9 0.6 %copy-done.6 = f32[2,8,640]{2,1,0:T(8,128)} copy-done((f32[2,8,640]{2,1,0:T(8,128)}, f32[2,8,640]{2,1,0:T(8,128)S(1)}, u32[]{:S(2)}) %copy-start.6) | copy-done | bytes 40984
  17.5 0.0 copy-done.7
  17.5 1.5 %rims_by_side.1 = (f32[4,8,640]{2,1,0:T(8,128)}, f32[4,8,640]{2,1,0:T(8,128)}) custom-call(f32[2,8,640]{2,1,0:T(8,128)} %get-tuple-element.21.refs_0_, f32[2,8,640]{2,1,0:T(8,128)} %copy-done.5, f32[2,8,640]{2,1,0:T(8,128)} %copy-done.6, f32[2,8,640]{2,1,0:T(8,128)} %copy-done.7), custom_call_target="tpu_custom_call" | custom-call | tf_op jit(solution)/shard_map/rims_by_side/pallas_call | solution.py:141
  19.1 3.7 %collective-permute-start.3 = (f32[4,8,640]{2,1,0:T(8,128)}, f32[4,8,640]{2,1,0:T(8,128)S(1)}, u32[]{:S(2)}, u32[]{:S(2)}) collective-permute-start(f32[4,8,640]{2,1,0:T(8,128)} %get-tuple-element.25), channel_id=1, source_target_pairs={{0,1},{1,2},{2,3},{4,5},{5,6},{6,7},{8,9},{9,10},{10,11},{12,13},{... | collective-permute-start | bytes 245768 | tf_op jit(solution)/shard_map/ppermute | solution.py:355
  22.8 1.3 %collective-permute-start.4 = (f32[4,8,640]{2,1,0:T(8,128)}, f32[4,8,640]{2,1,0:T(8,128)S(1)}, u32[]{:S(2)}, u32[]{:S(2)}) collective-permute-start(f32[4,8,640]{2,1,0:T(8,128)} %get-tuple-element.26), channel_id=1, source_target_pairs={{1,0},{2,1},{3,2},{5,4},{6,5},{7,6},{9,8},{10,9},{11,10},{13,12},{... | collective-permute-start | bytes 245768 | tf_op jit(solution)/shard_map/ppermute | solution.py:354
  24.1 1.9 %angle_weights.1 = (bf16[2,128,256]{2,1,0:T(8,128)(2,1)}, s32[8,128]{1,0:T(8,128)}) custom-call(s32[1,128]{1,0:T(1,128)} %bitcast.1, f32[128,128]{1,0:T(8,128)} %map_ref.1), custom_call_target="tpu_custom_call" | custom-call | tf_op jit(solution)/shard_map/angle_weights/pallas_call | solution.py:171
  26.0 0.0 collective-permute-done.3.refs_3_
  26.0 0.0 copy-start.3
  26.0 3.4 %collective-permute-done.4.refs_4_ = f32[4,8,640]{2,1,0:T(8,128)S(1)} collective-permute-done((f32[4,8,640]{2,1,0:T(8,128)}, f32[4,8,640]{2,1,0:T(8,128)S(1)}, u32[]{:S(2)}, u32[]{:S(2)}) %collective-permute-start.4) | collective-permute-done | bytes 81952 | tf_op jit(solution)/shard_map/ppermute | solution.py:354
  29.3 0.0 copy-start.4
  29.3 0.0 collective-permute-done.5.refs_6_
  29.3 0.0 copy-start
  29.3 0.0 collective-permute-done.6.refs_7_
  29.3 0.0 copy-start.1
  29.4 0.0 collective-permute-done.7.refs_8_
  29.4 0.0 copy-start.2
  29.4 0.0 copy-done.3
  29.4 0.6 %copy-done.4 = f32[4,8,640]{2,1,0:T(8,128)} copy-done((f32[4,8,640]{2,1,0:T(8,128)}, f32[4,8,640]{2,1,0:T(8,128)S(1)}, u32[]{:S(2)}) %copy-start.4) | copy-done | bytes 81944
  30.0 0.1 copy-done
  30.0 0.0 copy-done.1
  30.1 0.1 copy-done.2
  30.2 10.7 %angle_image.1 = f32[128,32,512]{2,1,0:T(8,128)} custom-call(s32[8,128]{1,0:T(8,128)} %get-tuple-element.18.refs_0_, bf16[2,128,256]{2,1,0:T(8,128)(2,1)} %get-tuple-element.19.refs_1_, f32[2,16,640]{2,1,0:T(8,128)} %get-tuple-element.20.refs_2_, f32[4,8,640]{2,1,0:T(8,128)} %copy-done.3, f32[4,8,640]{2,1,0:T(8,128)} %copy-done.4, ...), custom_call_target="tpu_custom_call" | custom-call | tf_op jit(solution)/shard_map/angle_image/pallas_call | solution.py:314
Async XLA Ops:
  3.9 4.9 %collective-permute-start = (f32[2,8,640]{2,1,0:T(8,128)}, f32[2,8,640]{2,1,0:T(8,128)S(1)}, u32[]{:S(2)}, u32[]{:S(2)}) collective-permute-start(f32[2,8,640]{2,1,0:T(8,128)} %get-tuple-element.22), channel_id=1, source_target_pairs={{0,4},{4,0},{8,12},{12,8},{1,5},{5,1},{9,13},{13,9},{2,6},{6,2},{1... | collective-permute-start | bytes 122888 | tf_op jit(solution)/shard_map/ppermute | solution.py:347
  4.4 24.9 %collective-permute-start.5 = (f32[2,32,640]{2,1,0:T(8,128)}, f32[2,32,640]{2,1,0:T(8,128)S(1)}, u32[]{:S(2)}, u32[]{:S(2)}) collective-permute-start(f32[2,32,640]{2,1,0:T(8,128)} %get-tuple-element.28), channel_id=1, source_target_pairs={{0,4},{4,0},{8,12},{12,8},{1,5},{5,1},{9,13},{13,9},{2,6},{6,2},{1... | collective-permute-start | bytes 491528 | tf_op jit(solution)/shard_map/ppermute | solution.py:347
  4.5 24.8 %collective-permute-start.6 = (f32[2,32,640]{2,1,0:T(8,128)}, f32[2,32,640]{2,1,0:T(8,128)S(1)}, u32[]{:S(2)}, u32[]{:S(2)}) collective-permute-start(f32[2,32,640]{2,1,0:T(8,128)} %get-tuple-element.29), channel_id=1, source_target_pairs={{0,8},{4,12},{8,0},{12,4},{1,9},{5,13},{9,1},{13,5},{2,10},{6,14},... | collective-permute-start | bytes 491528 | tf_op jit(solution)/shard_map/ppermute | solution.py:347
  7.4 21.9 %collective-permute-start.7 = (f32[2,32,640]{2,1,0:T(8,128)}, f32[2,32,640]{2,1,0:T(8,128)S(1)}, u32[]{:S(2)}, u32[]{:S(2)}) collective-permute-start(f32[2,32,640]{2,1,0:T(8,128)} %get-tuple-element.30), channel_id=1, source_target_pairs={{0,12},{4,8},{8,4},{12,0},{1,13},{5,9},{9,5},{13,1},{2,14},{6,10},... | collective-permute-start | bytes 491528 | tf_op jit(solution)/shard_map/ppermute | solution.py:347
  7.4 9.5 %collective-permute-start.1 = (f32[2,8,640]{2,1,0:T(8,128)}, f32[2,8,640]{2,1,0:T(8,128)S(1)}, u32[]{:S(2)}, u32[]{:S(2)}) collective-permute-start(f32[2,8,640]{2,1,0:T(8,128)} %get-tuple-element.23), channel_id=1, source_target_pairs={{0,8},{4,12},{8,0},{12,4},{1,9},{5,13},{9,1},{13,5},{2,10},{6,14},... | collective-permute-start | bytes 122888 | tf_op jit(solution)/shard_map/ppermute | solution.py:347
  8.8 8.1 %copy-start.5 = (f32[2,8,640]{2,1,0:T(8,128)}, f32[2,8,640]{2,1,0:T(8,128)S(1)}, u32[]{:S(2)}) copy-start(f32[2,8,640]{2,1,0:T(8,128)S(1)} %collective-permute-done.refs_1_) | copy-start | bytes 122884
  8.8 8.0 %collective-permute-start.2 = (f32[2,8,640]{2,1,0:T(8,128)}, f32[2,8,640]{2,1,0:T(8,128)S(1)}, u32[]{:S(2)}, u32[]{:S(2)}) collective-permute-start(f32[2,8,640]{2,1,0:T(8,128)} %get-tuple-element.24), channel_id=1, source_target_pairs={{0,12},{4,8},{8,4},{12,0},{1,13},{5,9},{9,5},{13,1},{2,14},{6,10},... | collective-permute-start | bytes 122888 | tf_op jit(solution)/shard_map/ppermute | solution.py:347
  16.9 0.6 %copy-start.6 = (f32[2,8,640]{2,1,0:T(8,128)}, f32[2,8,640]{2,1,0:T(8,128)S(1)}, u32[]{:S(2)}) copy-start(f32[2,8,640]{2,1,0:T(8,128)S(1)} %collective-permute-done.1.refs_2_) | copy-start | bytes 122884
  16.9 0.6 %copy-start.7 = (f32[2,8,640]{2,1,0:T(8,128)}, f32[2,8,640]{2,1,0:T(8,128)S(1)}, u32[]{:S(2)}) copy-start(f32[2,8,640]{2,1,0:T(8,128)S(1)} %collective-permute-done.2.refs_3_) | copy-start | bytes 122884
  19.1 6.9 %collective-permute-start.3 = (f32[4,8,640]{2,1,0:T(8,128)}, f32[4,8,640]{2,1,0:T(8,128)S(1)}, u32[]{:S(2)}, u32[]{:S(2)}) collective-permute-start(f32[4,8,640]{2,1,0:T(8,128)} %get-tuple-element.25), channel_id=1, source_target_pairs={{0,1},{1,2},{2,3},{4,5},{5,6},{6,7},{8,9},{9,10},{10,11},{12,13},{... | collective-permute-start | bytes 245768 | tf_op jit(solution)/shard_map/ppermute | solution.py:355
  22.8 6.5 %collective-permute-start.4 = (f32[4,8,640]{2,1,0:T(8,128)}, f32[4,8,640]{2,1,0:T(8,128)S(1)}, u32[]{:S(2)}, u32[]{:S(2)}) collective-permute-start(f32[4,8,640]{2,1,0:T(8,128)} %get-tuple-element.26), channel_id=1, source_target_pairs={{1,0},{2,1},{3,2},{5,4},{6,5},{7,6},{9,8},{10,9},{11,10},{13,12},{... | collective-permute-start | bytes 245768 | tf_op jit(solution)/shard_map/ppermute | solution.py:354
  26.0 3.4 %copy-start.3 = (f32[4,8,640]{2,1,0:T(8,128)}, f32[4,8,640]{2,1,0:T(8,128)S(1)}, u32[]{:S(2)}) copy-start(f32[4,8,640]{2,1,0:T(8,128)S(1)} %collective-permute-done.3.refs_3_) | copy-start | bytes 245764
  29.3 0.6 %copy-start.4 = (f32[4,8,640]{2,1,0:T(8,128)}, f32[4,8,640]{2,1,0:T(8,128)S(1)}, u32[]{:S(2)}) copy-start(f32[4,8,640]{2,1,0:T(8,128)S(1)} %collective-permute-done.4.refs_4_) | copy-start | bytes 245764
  29.3 0.7 %copy-start = (f32[2,32,640]{2,1,0:T(8,128)}, f32[2,32,640]{2,1,0:T(8,128)S(1)}, u32[]{:S(2)}) copy-start(f32[2,32,640]{2,1,0:T(8,128)S(1)} %collective-permute-done.5.refs_6_) | copy-start | bytes 491524
  29.3 0.7 %copy-start.1 = (f32[2,32,640]{2,1,0:T(8,128)}, f32[2,32,640]{2,1,0:T(8,128)S(1)}, u32[]{:S(2)}) copy-start(f32[2,32,640]{2,1,0:T(8,128)S(1)} %collective-permute-done.6.refs_7_) | copy-start | bytes 491524
  29.4 0.8 %copy-start.2 = (f32[2,32,640]{2,1,0:T(8,128)}, f32[2,32,640]{2,1,0:T(8,128)S(1)}, u32[]{:S(2)}) copy-start(f32[2,32,640]{2,1,0:T(8,128)S(1)} %collective-permute-done.7.refs_8_) | copy-start | bytes 491524

commit v4 on v3

--- a/solution.py
+++ b/solution.py
@@ -16,6 +16,7 @@
 MB = 4
 NB = 4
 APART = 16
+
 
 coeffs = (-205.0 / 72.0, 8.0 / 5.0, -1.0 / 5.0, 8.0 / 315.0, -1.0 / 560.0)
 
@@ -41,9 +42,9 @@
 
 
 def step_body(width, cell_ref, amp_ref, src_now, src_prev, rcv_now, rcv_prev, courant, speed_ref, *refs):
-    count = (len(refs) - 4) // 2
-    rims, wins = refs[:count], refs[count : 2 * count]
-    rows_ref, padded, padded_rim, padded_speed = refs[2 * count :]
+    count = (len(refs) - 4) // 3
+    tops, bottoms, wins = refs[:count], refs[count : 2 * count], refs[2 * count : 3 * count]
+    rows_ref, padded, padded_rim, padded_speed = refs[3 * count :]
     depth, nx = src_now.shape[1:]
     blocks = nx // LANES
     me = lax.axis_index("offset")
@@ -98,7 +99,8 @@
         other = lax.bitwise_xor(me, d)
         for f, first in enumerate((count - 1 - other, other)):
             at = pl.ds(pl.multiple_of(first * width, LANES), width + 2 * MAXLAG)
-            rims[d][f] = padded_rim[f, :, at]
+            tops[d][f] = padded_rim[f, :RIM, at]
+            bottoms[d][f] = padded_rim[f, RIM:, at]
             wins[d][f] = padded[f, :, at]
             if d == 0:
                 speed_ref[f] = padded_speed[f, :, at]
@@ -113,8 +115,8 @@
     speed, *rest = pl.pallas_call(
         functools.partial(step_body, width),
         in_specs=[smem, smem] + [vmem] * len(fields),
-        out_specs=[vmem] * (1 + 2 * count),
-        out_shape=[shape(2 * GROUP)] + [shape(GROUP)] * count + [shape(depth)] * count,
+        out_specs=[vmem] * (1 + 3 * count),
+        out_shape=[shape(2 * GROUP)] + [shape(RIM)] * (2 * count) + [shape(depth)] * count,
         scratch_shapes=[
             pltpu.VMEM((2, nx // LANES, depth + 2 * GROUP, LANES), jnp.float32),
             pltpu.VMEM((2, depth, nx + 2 * MAXLAG), jnp.float32),
@@ -124,26 +126,7 @@
         compiler_params=pltpu.CompilerParams(vmem_limit_bytes=60 << 20),
         name="step",
     )(cell, amp, *fields)
-    return speed, rest[:count], rest[count:]
-
-
-def rim_body(*refs):
-    shots = len(refs) - 2
-    up_ref, down_ref = refs[shots:]
-    for s in range(shots):
-        for f in range(2):
-            up_ref[s, f * RIM : (f + 1) * RIM, :] = refs[s][f, :RIM, :]
-            down_ref[s, f * RIM : (f + 1) * RIM, :] = refs[s][f, RIM:, :]
-
-
-def rims_by_side(rims):
-    out = jax.ShapeDtypeStruct((len(rims), 2 * RIM, rims[0].shape[2]), jnp.float32)
-    return pl.pallas_call(
-        rim_body,
-        out_shape=[out, out],
-        compiler_params=pltpu.CompilerParams(vmem_limit_bytes=60 << 20),
-        name="rims_by_side",
-    )(*rims)
+    return speed, rest[:count], rest[count : 2 * count], rest[2 * count :]
 
 
 def weight_body(shift_ref, map_ref, mw_ref, slot_ref):
@@ -235,10 +218,10 @@
 
 
 def image_body(blocks, shots, *refs):
-    given, out_ref = refs[: 5 + shots], refs[5 + shots]
-    slot_ref, mw_ref, speed, above, below, held, ext, fwd, rev, obuf, stage, in_sems, out_sems = refs[6 + shots :]
+    given, out_ref = refs[: 3 + 3 * shots], refs[3 + 3 * shots]
+    slot_ref, mw_ref, speed, above, below, held, ext, fwd, rev, obuf, stage, in_sems, out_sems = refs[4 + 3 * shots :]
     na, depth, _ = out_ref.shape
-    kept = [slot_ref, mw_ref, speed, above, below] + [held.at[s] for s in range(shots)]
+    kept = [slot_ref, mw_ref, speed] + [x.at[s] for x in (above, below, held) for s in range(shots)]
     fetches = [pltpu.make_async_copy(x, y, in_sems.at[i]) for i, (x, y) in enumerate(zip(given, kept))]
     for fetch in fetches:
         fetch.start()
@@ -249,15 +232,14 @@
     low = depth - GROUP
     for s in range(shots):
         for f in range(2):
-            rim = slice(f * RIM, (f + 1) * RIM)
             for t in range(blocks + 1):
                 at = slice(t * LANES, (t + 1) * LANES)
                 ext[s, f, t, 0:GROUP, :] = zero
                 ext[s, f, t, GROUP : 2 * GROUP, :] = zero
                 ext[s, f, t, 2 * GROUP : 3 * GROUP, :] = zero
                 ext[s, f, t, 3 * GROUP : 4 * GROUP, :] = zero
-                ext[s, f, t, GROUP - RIM : GROUP, :] = above[s, rim, at]
-                ext[s, f, t, 3 * GROUP : 3 * GROUP + RIM, :] = below[s, rim, at]
+                ext[s, f, t, GROUP - RIM : GROUP, :] = above[s, f, :, at]
+                ext[s, f, t, 3 * GROUP : 3 * GROUP + RIM, :] = below[s, f, :, at]
                 top, bottom = None, None
                 for k in range(1, RIM + 1):
                     u = coeffs[k] * ext[s, f, t, GROUP - k : 2 * GROUP - k, :]
@@ -314,26 +296,26 @@
     return pl.pallas_call(
         functools.partial(image_body, width // LANES, shots),
         out_shape=jax.ShapeDtypeStruct((na, depth, width), jnp.float32),
-        in_specs=[anywhere] * (5 + shots),
+        in_specs=[anywhere] * (3 + 3 * shots),
         out_specs=pl.BlockSpec(memory_space=pltpu.HBM),
         scratch_shapes=[
             like(slot),
             like(mw),
             like(speed),
-            like(above),
-            like(below),
+            pltpu.VMEM((shots, *above[0].shape), jnp.float32),
+            pltpu.VMEM((shots, *below[0].shape), jnp.float32),
             pltpu.VMEM((shots, *wins[0].shape), jnp.float32),
             pltpu.VMEM((shots, 2, full // LANES, 4 * GROUP, LANES), jnp.float32),
             pltpu.VMEM((shots, ROWS, LANES), jnp.float32),
             pltpu.VMEM((shots, ROWS, LANES), jnp.float32),
             pltpu.VMEM((na * PITCH, LANES), jnp.float32),
             pltpu.VMEM((na, depth, width), jnp.float32),
-            pltpu.SemaphoreType.DMA((5 + shots,)),
+            pltpu.SemaphoreType.DMA((3 + 3 * shots,)),
             pltpu.SemaphoreType.DMA((na // APART,)),
         ],
         compiler_params=pltpu.CompilerParams(vmem_limit_bytes=60 << 20),
         name="angle_image",
-    )(slot, mw, speed, above, below, *wins)
+    )(slot, mw, speed, *above, *below, *wins)
 
 
 def body(src_now, src_prev, rcv_now, rcv_prev, courant, shot_cell, wavelet, shifts, angle_map):
@@ -347,12 +329,24 @@
             out.append(lax.ppermute(parts[d], "offset", [(i, i ^ d) for i in range(count)]))
         return out
 
-    speed, rims, wins = stepped_windows(count, shot_cell, wavelet, (src_now, src_prev, rcv_now, rcv_prev, courant))
-    rims = exchanged(rims)
+    def from_slab(parts, side):
+        out = []
+        for d in range(count):
+            pairs = [
+                (i * slabs + z, (i ^ d) * slabs + z + side)
+                for z in range(slabs)
+                if 0 <= z + side < slabs
+                for i in range(count)
+            ]
+            out.append(lax.ppermute(parts[d], ("offset", "space"), pairs))
+        return out
+
+    speed, tops, bottoms, wins = stepped_windows(
+        count, shot_cell, wavelet, (src_now, src_prev, rcv_now, rcv_prev, courant)
+    )
     wins = exchanged(wins)
-    up, down = rims_by_side(rims)
-    below = lax.ppermute(up, "space", [(i + 1, i) for i in range(slabs - 1)])
-    above = lax.ppermute(down, "space", [(i, i + 1) for i in range(slabs - 1)])
+    below = from_slab(tops, -1)
+    above = from_slab(bottoms, 1)
     mw, slot = angle_weights(shifts, angle_map)
     return angle_image(wins, above, below, speed, mw, slot, depth)
 

time: 41.1 us -> 46.7 us (1.14); the launches traced: 40.8 us -> 45.8 us
  starting transfers between devices: 10.3 us -> 21.5 us
  waiting for transfers between devices: 11 us -> 6.88 us
  Pallas kernels: 18 us -> 16.5 us
  local copies, waits for them, and re-layouts: 1.41 us -> 0.73 us
    ppermute x2 -> x8, starting transfers between devices: 5.01 us -> 18.4 us  [from_slab(): out.append(lax.ppermute(parts[d], ('offset', 'space'), pairs))]
    ppermute x6 -> x3, waiting for transfers between devices: 7.65 us -> 0.01 us  [exchanged(): lax.ppermute(parts[d], 'offset', [(i, i ^ d) for i in range(count)])]
    ppermute x2 -> x8, waiting for transfers between devices: 3.37 us -> 6.88 us  [from_slab(): out.append(lax.ppermute(parts[d], ('offset', 'space'), pairs))]
    ppermute x6 -> x3, starting transfers between devices: 5.3 us -> 3.09 us  [exchanged(): lax.ppermute(parts[d], 'offset', [(i, i ^ d) for i in range(count)])]
    pallas_call x1 -> x0, Pallas kernels: 1.54 us -> none  [rims_by_side(): pl.pallas_call(rim_body, out_shape=[out, out], compiler_params=pltpu.Comp...]
    unnamed x16 -> x22, local copies, waits for them, and re-layouts: 1.41 us -> 0.73 us
  transfers between devices with their start and end apart: 8 -> 11, of which waited for: 2 -> 5; matrix products, arithmetic and copies ran while one was open for 0% -> 0% of each run, Pallas kernels for 8% -> 4%
where the time goes in v4:
time: 46.7 us; the launch traced here: 45.8 us
  starting transfers between devices  21.5 us (46%)
  Pallas kernels  16.5 us (35%)
  waiting for transfers between devices  6.88 us (15%)
  local copies, waits for them, and re-layouts  0.73 us (2%)
    ppermute x8, starting transfers between devices, from_slab(): out.append(lax.ppermute(parts[d], ('offset', 'space'), pairs))  18.4 us
    pallas_call x1, Pallas kernels, angle_image(): pl.pallas_call(functools.partial(image_body, width // LANES, shots), out_...  10.8 us
    ppermute x8, waiting for transfers between devices, from_slab(): out.append(lax.ppermute(parts[d], ('offset', 'space'), pairs))  6.88 us
    pallas_call x1, Pallas kernels, stepped_windows(): pl.pallas_call(functools.partial(step_body, width), in_specs=[smem, smem]...  3.92 us
    ppermute x3, starting transfers between devices, exchanged(): lax.ppermute(parts[d], 'offset', [(i, i ^ d) for i in range(count)])  3.09 us
    pallas_call x1, Pallas kernels, angle_weights(): pl.pallas_call(weight_body, out_shape=[jax.ShapeDtypeStruct((2, na, ROWS)...  1.85 us
  transfers between devices with their start and end apart: 11, of which 5 were waited for; matrix products, arithmetic and copies ran while one was open for 0% of the time, Pallas kernels for 4%

profile of v4, /device:TPU:0, one launch (start us, length us, event | category | flops | bytes accessed | tf_op | source)
XLA Modules:
  0.0 45.8 jit_solution(13139470636422658003)
XLA Ops:
  0.0 3.9 %step.1 = (f32[2,16,640]{2,1,0:T(8,128)}, f32[2,4,640]{2,1,0:T(4,128)}, f32[2,4,640]{2,1,0:T(4,128)}, f32[2,4,640]{2,1,0:T(4,128)}, f32[2,4,640]{2,1,0:T(4,128)}...) custom-call(s32[4]{0:T(128)} %cell_ref.1, ...), custom_call_target="tpu_custom_call" | custom-call | tf_op jit(solution)/shard_map/step/pallas_call | solution.py:115
  3.9 0.5 %collective-permute-start.8 = (f32[2,32,640]{2,1,0:T(8,128)}, f32[2,32,640]{2,1,0:T(8,128)S(1)}, u32[]{:S(2)}, u32[]{:S(2)}) collective-permute-start(f32[2,32,640]{2,1,0:T(8,128)} %get-tuple-element.32), channel_id=1, source_target_pairs={{0,4},{4,0},{8,12},{12,8},{1,5},{5,1},{9,13},{13,9},{2,6},{6,2},{1... | collective-permute-start | bytes 491528 | tf_op jit(solution)/shard_map/ppermute | solution.py:329
  4.4 2.5 %collective-permute-start.9 = (f32[2,32,640]{2,1,0:T(8,128)}, f32[2,32,640]{2,1,0:T(8,128)S(1)}, u32[]{:S(2)}, u32[]{:S(2)}) collective-permute-start(f32[2,32,640]{2,1,0:T(8,128)} %get-tuple-element.33), channel_id=1, source_target_pairs={{0,8},{4,12},{8,0},{12,4},{1,9},{5,13},{9,1},{13,5},{2,10},{6,14},... | collective-permute-start | bytes 491528 | tf_op jit(solution)/shard_map/ppermute | solution.py:329
  7.0 0.0 collective-permute-start.10
  7.0 3.7 %collective-permute-start = (f32[2,4,640]{2,1,0:T(4,128)}, f32[2,4,640]{2,1,0:T(4,128)S(1)}, u32[]{:S(2)}, u32[]{:S(2)}) collective-permute-start(f32[2,4,640]{2,1,0:T(4,128)} %get-tuple-element.23), channel_id=1, source_target_pairs={{0,1},{4,5},{8,9},{12,13},{1,2},{5,6},{9,10},{13,14},{2,3},{6,7},{... | collective-permute-start | bytes 61448 | tf_op jit(solution)/shard_map/ppermute | solution.py:341
  10.7 3.2 %collective-permute-start.1 = (f32[2,4,640]{2,1,0:T(4,128)}, f32[2,4,640]{2,1,0:T(4,128)S(1)}, u32[]{:S(2)}, u32[]{:S(2)}) collective-permute-start(f32[2,4,640]{2,1,0:T(4,128)} %get-tuple-element.24), channel_id=1, source_target_pairs={{0,5},{4,1},{8,13},{12,9},{1,6},{5,2},{9,14},{13,10},{2,7},{6,3},{... | collective-permute-start | bytes 61448 | tf_op jit(solution)/shard_map/ppermute | solution.py:341
  13.9 0.0 collective-permute-done.refs_3_
  13.9 0.0 copy-start.3
  13.9 4.4 %collective-permute-start.2 = (f32[2,4,640]{2,1,0:T(4,128)}, f32[2,4,640]{2,1,0:T(4,128)S(1)}, u32[]{:S(2)}, u32[]{:S(2)}) collective-permute-start(f32[2,4,640]{2,1,0:T(4,128)} %get-tuple-element.25), channel_id=1, source_target_pairs={{0,9},{4,13},{8,1},{12,5},{1,10},{5,14},{9,2},{13,6},{2,11},{6,15}... | collective-permute-start | bytes 61448 | tf_op jit(solution)/shard_map/ppermute | solution.py:341
  18.3 0.0 collective-permute-done.1.refs_4_
  18.4 0.0 copy-start.4
  18.4 2.0 %collective-permute-start.3 = (f32[2,4,640]{2,1,0:T(4,128)}, f32[2,4,640]{2,1,0:T(4,128)S(1)}, u32[]{:S(2)}, u32[]{:S(2)}) collective-permute-start(f32[2,4,640]{2,1,0:T(4,128)} %get-tuple-element.26), channel_id=1, source_target_pairs={{0,13},{4,9},{8,5},{12,1},{1,14},{5,10},{9,6},{13,2},{2,15},{6,11}... | collective-permute-start | bytes 61448 | tf_op jit(solution)/shard_map/ppermute | solution.py:341
  20.3 0.0 collective-permute-done.2.refs_5_
  20.4 0.0 copy-start.5
  20.4 1.3 %collective-permute-start.4 = (f32[2,4,640]{2,1,0:T(4,128)}, f32[2,4,640]{2,1,0:T(4,128)S(1)}, u32[]{:S(2)}, u32[]{:S(2)}) collective-permute-start(f32[2,4,640]{2,1,0:T(4,128)} %get-tuple-element.27), channel_id=1, source_target_pairs={{1,0},{5,4},{9,8},{13,12},{2,1},{6,5},{10,9},{14,13},{3,2},{7,6},{... | collective-permute-start | bytes 61448 | tf_op jit(solution)/shard_map/ppermute | solution.py:341
  21.7 0.4 collective-permute-done.3.refs_6_
  22.0 0.0 copy-start.6
  22.0 1.3 %collective-permute-start.5 = (f32[2,4,640]{2,1,0:T(4,128)}, f32[2,4,640]{2,1,0:T(4,128)S(1)}, u32[]{:S(2)}, u32[]{:S(2)}) collective-permute-start(f32[2,4,640]{2,1,0:T(4,128)} %get-tuple-element.28), channel_id=1, source_target_pairs={{1,4},{5,0},{9,12},{13,8},{2,5},{6,1},{10,13},{14,9},{3,6},{7,2},{... | collective-permute-start | bytes 61448 | tf_op jit(solution)/shard_map/ppermute | solution.py:341
  23.3 3.0 %collective-permute-done.4.refs_7_ = f32[2,4,640]{2,1,0:T(4,128)S(1)} collective-permute-done((f32[2,4,640]{2,1,0:T(4,128)}, f32[2,4,640]{2,1,0:T(4,128)S(1)}, u32[]{:S(2)}, u32[]{:S(2)}) %collective-permute-start.4) | collective-permute-done | bytes 20512 | tf_op jit(solution)/shard_map/ppermute | solution.py:341
  26.3 0.0 copy-start.7
  26.3 1.3 %collective-permute-start.6 = (f32[2,4,640]{2,1,0:T(4,128)}, f32[2,4,640]{2,1,0:T(4,128)S(1)}, u32[]{:S(2)}, u32[]{:S(2)}) collective-permute-start(f32[2,4,640]{2,1,0:T(4,128)} %get-tuple-element.29), channel_id=1, source_target_pairs={{1,8},{5,12},{9,0},{13,4},{2,9},{6,13},{10,1},{14,5},{3,10},{7,14}... | collective-permute-start | bytes 61448 | tf_op jit(solution)/shard_map/ppermute | solution.py:341
  27.6 0.4 collective-permute-done.5.refs_8_
  28.0 0.0 copy-start.8
  28.0 1.3 %collective-permute-start.7 = (f32[2,4,640]{2,1,0:T(4,128)}, f32[2,4,640]{2,1,0:T(4,128)S(1)}, u32[]{:S(2)}, u32[]{:S(2)}) collective-permute-start(f32[2,4,640]{2,1,0:T(4,128)} %get-tuple-element.30), channel_id=1, source_target_pairs={{1,12},{5,8},{9,4},{13,0},{2,13},{6,9},{10,5},{14,1},{3,14},{7,10}... | collective-permute-start | bytes 61448 | tf_op jit(solution)/shard_map/ppermute | solution.py:341
  29.3 1.9 %angle_weights.1 = (bf16[2,128,256]{2,1,0:T(8,128)(2,1)}, s32[8,128]{1,0:T(8,128)}) custom-call(s32[1,128]{1,0:T(1,128)} %bitcast.1, f32[128,128]{1,0:T(8,128)} %map_ref.1), custom_call_target="tpu_custom_call" | custom-call | tf_op jit(solution)/shard_map/angle_weights/pallas_call | solution.py:154
  31.2 1.9 %collective-permute-done.6.refs_9_ = f32[2,4,640]{2,1,0:T(4,128)S(1)} collective-permute-done((f32[2,4,640]{2,1,0:T(4,128)}, f32[2,4,640]{2,1,0:T(4,128)S(1)}, u32[]{:S(2)}, u32[]{:S(2)}) %collective-permute-start.6) | collective-permute-done | bytes 20512 | tf_op jit(solution)/shard_map/ppermute | solution.py:341
  33.1 0.0 copy-start.9
  33.1 1.2 %collective-permute-done.7.refs_10_ = f32[2,4,640]{2,1,0:T(4,128)S(1)} collective-permute-done((f32[2,4,640]{2,1,0:T(4,128)}, f32[2,4,640]{2,1,0:T(4,128)S(1)}, u32[]{:S(2)}, u32[]{:S(2)}) %collective-permute-start.7) | collective-permute-done | bytes 20512 | tf_op jit(solution)/shard_map/ppermute | solution.py:341
  34.3 0.0 copy-start.10
  34.3 0.0 collective-permute-done.8.refs_12_
  34.3 0.0 copy-start
  34.3 0.0 collective-permute-done.9.refs_13_
  34.3 0.0 copy-start.1
  34.3 0.0 collective-permute-done.10.refs_14_
  34.3 0.0 copy-start.2
  34.3 0.0 copy-done.3
  34.3 0.0 copy-done.4
  34.3 0.0 copy-done.5
  34.3 0.0 copy-done.6
  34.3 0.0 copy-done.7
  34.4 0.0 copy-done.8
  34.4 0.0 copy-done.9
  34.4 0.5 %copy-done.10 = f32[2,4,640]{2,1,0:T(4,128)} copy-done((f32[2,4,640]{2,1,0:T(4,128)}, f32[2,4,640]{2,1,0:T(4,128)S(1)}, u32[]{:S(2)}) %copy-start.10) | copy-done | bytes 20504
  34.9 0.1 copy-done
  34.9 0.1 copy-done.1
  35.0 0.1 copy-done.2
  35.1 10.8 %angle_image.1 = f32[128,32,512]{2,1,0:T(8,128)} custom-call(s32[8,128]{1,0:T(8,128)} %get-tuple-element.20.refs_0_, bf16[2,128,256]{2,1,0:T(8,128)(2,1)} %get-tuple-element.21.refs_1_, f32[2,16,640]{2,1,0:T(8,128)} %get-tuple-element.22.refs_2_, f32[2,4,640]{2,1,0:T(4,128)} %copy-done.3, f32[2,4,640]{2,1,0:T(4,128)} %copy-done.4, f32[2,4,640]{2,1,0:T(4,128)} %copy-done.5, ...), custom_call_target="tpu_custom_call" | custom-call | tf_op jit(solution)/shard_map/angle_image/pallas_call | solution.py:296
Async XLA Ops:
  3.9 30.3 %collective-permute-start.8 = (f32[2,32,640]{2,1,0:T(8,128)}, f32[2,32,640]{2,1,0:T(8,128)S(1)}, u32[]{:S(2)}, u32[]{:S(2)}) collective-permute-start(f32[2,32,640]{2,1,0:T(8,128)} %get-tuple-element.32), channel_id=1, source_target_pairs={{0,4},{4,0},{8,12},{12,8},{1,5},{5,1},{9,13},{13,9},{2,6},{6,2},{1... | collective-permute-start | bytes 491528 | tf_op jit(solution)/shard_map/ppermute | solution.py:329
  4.4 29.9 %collective-permute-start.9 = (f32[2,32,640]{2,1,0:T(8,128)}, f32[2,32,640]{2,1,0:T(8,128)S(1)}, u32[]{:S(2)}, u32[]{:S(2)}) collective-permute-start(f32[2,32,640]{2,1,0:T(8,128)} %get-tuple-element.33), channel_id=1, source_target_pairs={{0,8},{4,12},{8,0},{12,4},{1,9},{5,13},{9,1},{13,5},{2,10},{6,14},... | collective-permute-start | bytes 491528 | tf_op jit(solution)/shard_map/ppermute | solution.py:329
  7.0 27.3 %collective-permute-start.10 = (f32[2,32,640]{2,1,0:T(8,128)}, f32[2,32,640]{2,1,0:T(8,128)S(1)}, u32[]{:S(2)}, u32[]{:S(2)}) collective-permute-start(f32[2,32,640]{2,1,0:T(8,128)} %get-tuple-element.34), channel_id=1, source_target_pairs={{0,12},{4,8},{8,4},{12,0},{1,13},{5,9},{9,5},{13,1},{2,14},{6,10},... | collective-permute-start | bytes 491528 | tf_op jit(solution)/shard_map/ppermute | solution.py:329
  7.0 6.9 %collective-permute-start = (f32[2,4,640]{2,1,0:T(4,128)}, f32[2,4,640]{2,1,0:T(4,128)S(1)}, u32[]{:S(2)}, u32[]{:S(2)}) collective-permute-start(f32[2,4,640]{2,1,0:T(4,128)} %get-tuple-element.23), channel_id=1, source_target_pairs={{0,1},{4,5},{8,9},{12,13},{1,2},{5,6},{9,10},{13,14},{2,3},{6,7},{... | collective-permute-start | bytes 61448 | tf_op jit(solution)/shard_map/ppermute | solution.py:341
  10.7 7.6 %collective-permute-start.1 = (f32[2,4,640]{2,1,0:T(4,128)}, f32[2,4,640]{2,1,0:T(4,128)S(1)}, u32[]{:S(2)}, u32[]{:S(2)}) collective-permute-start(f32[2,4,640]{2,1,0:T(4,128)} %get-tuple-element.24), channel_id=1, source_target_pairs={{0,5},{4,1},{8,13},{12,9},{1,6},{5,2},{9,14},{13,10},{2,7},{6,3},{... | collective-permute-start | bytes 61448 | tf_op jit(solution)/shard_map/ppermute | solution.py:341
  13.9 20.4 %copy-start.3 = (f32[2,4,640]{2,1,0:T(4,128)}, f32[2,4,640]{2,1,0:T(4,128)S(1)}, u32[]{:S(2)}) copy-start(f32[2,4,640]{2,1,0:T(4,128)S(1)} %collective-permute-done.refs_3_) | copy-start | bytes 61444
  13.9 6.4 %collective-permute-start.2 = (f32[2,4,640]{2,1,0:T(4,128)}, f32[2,4,640]{2,1,0:T(4,128)S(1)}, u32[]{:S(2)}, u32[]{:S(2)}) collective-permute-start(f32[2,4,640]{2,1,0:T(4,128)} %get-tuple-element.25), channel_id=1, source_target_pairs={{0,9},{4,13},{8,1},{12,5},{1,10},{5,14},{9,2},{13,6},{2,11},{6,15}... | collective-permute-start | bytes 61448 | tf_op jit(solution)/shard_map/ppermute | solution.py:341
  18.4 16.0 %copy-start.4 = (f32[2,4,640]{2,1,0:T(4,128)}, f32[2,4,640]{2,1,0:T(4,128)S(1)}, u32[]{:S(2)}) copy-start(f32[2,4,640]{2,1,0:T(4,128)S(1)} %collective-permute-done.1.refs_4_) | copy-start | bytes 61444
  18.4 3.6 %collective-permute-start.3 = (f32[2,4,640]{2,1,0:T(4,128)}, f32[2,4,640]{2,1,0:T(4,128)S(1)}, u32[]{:S(2)}, u32[]{:S(2)}) collective-permute-start(f32[2,4,640]{2,1,0:T(4,128)} %get-tuple-element.26), channel_id=1, source_target_pairs={{0,13},{4,9},{8,5},{12,1},{1,14},{5,10},{9,6},{13,2},{2,15},{6,11}... | collective-permute-start | bytes 61448 | tf_op jit(solution)/shard_map/ppermute | solution.py:341
  20.4 14.0 %copy-start.5 = (f32[2,4,640]{2,1,0:T(4,128)}, f32[2,4,640]{2,1,0:T(4,128)S(1)}, u32[]{:S(2)}) copy-start(f32[2,4,640]{2,1,0:T(4,128)S(1)} %collective-permute-done.2.refs_5_) | copy-start | bytes 61444
  20.4 5.9 %collective-permute-start.4 = (f32[2,4,640]{2,1,0:T(4,128)}, f32[2,4,640]{2,1,0:T(4,128)S(1)}, u32[]{:S(2)}, u32[]{:S(2)}) collective-permute-start(f32[2,4,640]{2,1,0:T(4,128)} %get-tuple-element.27), channel_id=1, source_target_pairs={{1,0},{5,4},{9,8},{13,12},{2,1},{6,5},{10,9},{14,13},{3,2},{7,6},{... | collective-permute-start | bytes 61448 | tf_op jit(solution)/shard_map/ppermute | solution.py:341
  22.0 12.3 %copy-start.6 = (f32[2,4,640]{2,1,0:T(4,128)}, f32[2,4,640]{2,1,0:T(4,128)S(1)}, u32[]{:S(2)}) copy-start(f32[2,4,640]{2,1,0:T(4,128)S(1)} %collective-permute-done.3.refs_6_) | copy-start | bytes 61444
  22.0 6.0 %collective-permute-start.5 = (f32[2,4,640]{2,1,0:T(4,128)}, f32[2,4,640]{2,1,0:T(4,128)S(1)}, u32[]{:S(2)}, u32[]{:S(2)}) collective-permute-start(f32[2,4,640]{2,1,0:T(4,128)} %get-tuple-element.28), channel_id=1, source_target_pairs={{1,4},{5,0},{9,12},{13,8},{2,5},{6,1},{10,13},{14,9},{3,6},{7,2},{... | collective-permute-start | bytes 61448 | tf_op jit(solution)/shard_map/ppermute | solution.py:341
  26.3 8.0 %copy-start.7 = (f32[2,4,640]{2,1,0:T(4,128)}, f32[2,4,640]{2,1,0:T(4,128)S(1)}, u32[]{:S(2)}) copy-start(f32[2,4,640]{2,1,0:T(4,128)S(1)} %collective-permute-done.4.refs_7_) | copy-start | bytes 61444
  26.3 6.8 %collective-permute-start.6 = (f32[2,4,640]{2,1,0:T(4,128)}, f32[2,4,640]{2,1,0:T(4,128)S(1)}, u32[]{:S(2)}, u32[]{:S(2)}) collective-permute-start(f32[2,4,640]{2,1,0:T(4,128)} %get-tuple-element.29), channel_id=1, source_target_pairs={{1,8},{5,12},{9,0},{13,4},{2,9},{6,13},{10,1},{14,5},{3,10},{7,14}... | collective-permute-start | bytes 61448 | tf_op jit(solution)/shard_map/ppermute | solution.py:341
  28.0 6.3 %copy-start.8 = (f32[2,4,640]{2,1,0:T(4,128)}, f32[2,4,640]{2,1,0:T(4,128)S(1)}, u32[]{:S(2)}) copy-start(f32[2,4,640]{2,1,0:T(4,128)S(1)} %collective-permute-done.5.refs_8_) | copy-start | bytes 61444
  28.0 6.2 %collective-permute-start.7 = (f32[2,4,640]{2,1,0:T(4,128)}, f32[2,4,640]{2,1,0:T(4,128)S(1)}, u32[]{:S(2)}, u32[]{:S(2)}) collective-permute-start(f32[2,4,640]{2,1,0:T(4,128)} %get-tuple-element.30), channel_id=1, source_target_pairs={{1,12},{5,8},{9,4},{13,0},{2,13},{6,9},{10,5},{14,1},{3,14},{7,10}... | collective-permute-start | bytes 61448 | tf_op jit(solution)/shard_map/ppermute | solution.py:341
  33.1 1.3 %copy-start.9 = (f32[2,4,640]{2,1,0:T(4,128)}, f32[2,4,640]{2,1,0:T(4,128)S(1)}, u32[]{:S(2)}) copy-start(f32[2,4,640]{2,1,0:T(4,128)S(1)} %collective-permute-done.6.refs_9_) | copy-start | bytes 61444
  34.3 0.6 %copy-start.10 = (f32[2,4,640]{2,1,0:T(4,128)}, f32[2,4,640]{2,1,0:T(4,128)S(1)}, u32[]{:S(2)}) copy-start(f32[2,4,640]{2,1,0:T(4,128)S(1)} %collective-permute-done.7.refs_10_) | copy-start | bytes 61444
  34.3 0.7 %copy-start = (f32[2,32,640]{2,1,0:T(8,128)}, f32[2,32,640]{2,1,0:T(8,128)S(1)}, u32[]{:S(2)}) copy-start(f32[2,32,640]{2,1,0:T(8,128)S(1)} %collective-permute-done.8.refs_12_) | copy-start | bytes 491524
  34.3 0.7 %copy-start.1 = (f32[2,32,640]{2,1,0:T(8,128)}, f32[2,32,640]{2,1,0:T(8,128)S(1)}, u32[]{:S(2)}) copy-start(f32[2,32,640]{2,1,0:T(8,128)S(1)} %collective-permute-done.9.refs_13_) | copy-start | bytes 491524
  34.3 0.8 %copy-start.2 = (f32[2,32,640]{2,1,0:T(8,128)}, f32[2,32,640]{2,1,0:T(8,128)S(1)}, u32[]{:S(2)}) copy-start(f32[2,32,640]{2,1,0:T(8,128)S(1)} %collective-permute-done.10.refs_14_) | copy-start | bytes 491524
